TPU v7x, 32 devices: a whole 2x2x4 slice. The times are simulated.
32 devices in a mesh: sec: 2 (over x), el: 16 (over z, y, core).
Axes of the slice: x: 2, y: 2, z: 4, core: 2. Of those that a mesh axis runs over, the one named last changes fastest.
Arguments:
- green_lesser: bfloat16 [2, 256, 64, 2, 128], P('sec', 'el'), may hold values from -6 to 6
- green_greater: bfloat16 [2, 256, 64, 2, 128], P('sec', 'el'), may hold values from -6 to 6
- coulomb: bfloat16 [2, 2, 256, 256], P('sec'), may hold values from -0.375 to 0.375
- pattern: int32 [2, 64], replicated, may hold values from 0 to 511, as said below
Outputs:
- polar: bfloat16 [2, 256, 64, 2, 128], P('sec', 'el')
- screened: bfloat16 [2, 256, 2, 256, 256], P('sec', 'el')
Inputs may be any that keep to these rules, and one draw needn't show every extreme that they name: `pattern`: each row lists 64 distinct tile positions in increasing order.
All inputs are finite; a program needn't handle non-finite values.
Results may differ from a plain program's by a relative error of at most 0.014.
Values may be sent and summed in bfloat16 or wider, within the bound.
A program may use at most 128 MiB of HBM per device.

v0:
```python
import functools

import jax
import jax.numpy as jnp
import numpy as np
from jax import lax
from jax.experimental import pallas as pl
from jax.experimental.pallas import tpu as pltpu
from jax.sharding import PartitionSpec as P

TR = 8
TC = 16
VMEM_LIMIT = 56 * 1024 * 1024


def halves(table):
    upper = table.astype(jnp.bfloat16)
    lower = (table - upper.astype(np.float32)).astype(jnp.bfloat16)
    return upper, lower


def tables(energies):
    length = 2 * energies
    phase = np.outer(np.arange(length), np.arange(energies)) % length
    phase = phase * (2.0 * np.pi / length)
    cosine = np.cos(phase).astype(np.float32)
    sine = np.sin(phase).astype(np.float32)
    real = np.stack([cosine, sine], axis=2).reshape(length, length)
    imag = np.stack([-sine, cosine], axis=2).reshape(length, length)
    forward = np.concatenate(halves(np.concatenate([real, imag], axis=0)), axis=1)
    out_r = np.concatenate([-sine.T, -cosine.T], axis=1)
    out_i = np.concatenate([cosine.T, -sine.T], axis=1)
    inverse = np.stack([out_r, out_i], axis=1).reshape(length, 2 * length)
    return jnp.asarray(forward), jnp.asarray(np.concatenate(halves(inverse), axis=1))


def dot32(a, b):
    return jnp.dot(a, b, preferred_element_type=jnp.float32)


def correlate_slot(factor, lesser, greater, forward_ref, inverse_ref):
    energies, _, width = lesser.shape
    length = 2 * energies
    joined = jnp.concatenate(
        [lesser.reshape(length, width), greater.reshape(length, width)], axis=1
    )
    z = dot32(forward_ref[:, :length], joined) + dot32(forward_ref[:, length:], joined)
    lr, gr = z[:length, :width], z[:length, width:]
    li, gi = z[length:, :width], z[length:, width:]
    product = jnp.concatenate([lr * gr + li * gi, li * gr - lr * gi], axis=0)
    high = product.astype(jnp.bfloat16)
    low = (product - high.astype(jnp.float32)).astype(jnp.bfloat16)
    depth = 2 * length
    first = dot32(inverse_ref[:, :depth], jnp.concatenate([high, low], axis=1))
    series = first[:, :width] + first[:, width:] + dot32(inverse_ref[:, depth:], high)
    return (series * factor).astype(jnp.bfloat16).reshape(energies, 2, width)


def exchange_kernel(
    owners,
    sections,
    factor,
    lesser_ref,
    greater_ref,
    coulomb_ref,
    forward_hbm,
    inverse_hbm,
    *refs,
):
    sides = 1 if sections == 2 else 2
    polar_ref = refs[0]
    beside_refs = refs[1 : 1 + sides]
    other_ref = refs[1 + sides]
    (
        x_ref,
        d_ref,
        forward_ref,
        inverse_ref,
        table_sem,
        in_send,
        in_recv,
        out_send,
        out_recv,
        side_send,
        side_recv,
        c_send,
        c_recv,
    ) = refs[2 + sides :]
    slots = x_ref.shape[0]
    local = polar_ref.shape[0]
    me = lax.axis_index("el")
    section = lax.axis_index("sec")
    mesh_id = pl.DeviceIdType.MESH
    if sections == 2:
        targets = [1 - section]
    else:
        targets = [
            lax.rem(section + 1, sections),
            lax.rem(section + sections - 1, sections),
        ]

    load_f = pltpu.make_async_copy(forward_hbm, forward_ref, table_sem.at[0])
    load_i = pltpu.make_async_copy(inverse_hbm, inverse_ref, table_sem.at[1])
    load_f.start()
    load_i.start()

    barrier = pltpu.get_barrier_semaphore()

    def greet(step, carry):
        peer = lax.rem(me + step, owners)
        pl.semaphore_signal(barrier, inc=1, device_id={"el": peer}, device_id_type=mesh_id)
        return carry

    lax.fori_loop(1, owners, greet, 0)
    for target in targets:
        pl.semaphore_signal(barrier, inc=1, device_id={"sec": target}, device_id_type=mesh_id)
    pl.semaphore_wait(barrier, owners - 1 + sides)

    def peer_at(turn):
        return lax.rem(me + 1 + turn, owners)

    mine = pl.ds(me * local, local)
    for slot in range(slots):
        for which, source in enumerate((lesser_ref, greater_ref)):

            def send(turn, carry, slot=slot, which=which, source=source):
                peer = peer_at(turn)
                pltpu.make_async_remote_copy(
                    src_ref=source.at[:, peer, slot],
                    dst_ref=x_ref.at[slot, which, mine],
                    send_sem=in_send.at[slot],
                    recv_sem=in_recv.at[slot],
                    device_id={"el": peer},
                    device_id_type=mesh_id,
                ).start()
                return carry

            pltpu.make_async_copy(
                source.at[:, me, slot], x_ref.at[slot, which, mine], in_recv.at[slot]
            ).start()
            lax.fori_loop(0, owners - 1, send, 0)

    shared = pltpu.make_async_remote_copy(
        src_ref=coulomb_ref.at[1],
        dst_ref=other_ref,
        send_sem=c_send,
        recv_sem=c_recv,
        device_id={"sec": targets[0]},
        device_id_type=mesh_id,
    )
    shared.start()
    load_f.wait()
    load_i.wait()

    def arrive(slot):
        whole = polar_ref.at[:, :, slot]
        pltpu.make_async_copy(whole, whole, out_recv.at[slot]).wait()

    def forward_copy(slot, side):
        return pltpu.make_async_remote_copy(
            src_ref=polar_ref.at[:, :, slot],
            dst_ref=beside_refs[side].at[:, :, slot],
            send_sem=side_send.at[side, slot],
            recv_sem=side_recv.at[side, slot],
            device_id={"sec": targets[side]},
            device_id_type=mesh_id,
        )

    def pass_on(slot):
        arrive(slot)
        for side in range(sides):
            forward_copy(slot, side).start()

    for slot in range(slots):
        whole = x_ref.at[slot]
        pltpu.make_async_copy(whole, whole, in_recv.at[slot]).wait()
        d_ref[slot] = correlate_slot(
            factor, x_ref[slot, 0], x_ref[slot, 1], forward_ref, inverse_ref
        )
        pltpu.make_async_copy(
            d_ref.at[slot, mine], polar_ref.at[:, me, slot], out_recv.at[slot]
        ).start()

        def give(turn, carry, slot=slot):
            peer = peer_at(turn)
            pltpu.make_async_remote_copy(
                src_ref=d_ref.at[slot, pl.ds(peer * local, local)],
                dst_ref=polar_ref.at[:, me, slot],
                send_sem=out_send.at[slot],
                recv_sem=out_recv.at[slot],
                device_id={"el": peer},
                device_id_type=mesh_id,
            ).start()
            return carry

        lax.fori_loop(0, owners - 1, give, 0)
        if slot >= 2:
            pass_on(slot - 2)
    for slot in range(max(slots - 2, 0), slots):
        pass_on(slot)

    sent = (owners - 1) * local
    for slot in range(slots):
        part = x_ref.at[slot, :, pl.ds(0, sent)]
        pltpu.make_async_copy(part, part, in_send.at[slot]).wait()
        part = d_ref.at[slot, pl.ds(0, sent)]
        pltpu.make_async_copy(part, part, out_send.at[slot]).wait()
        for side in range(sides):
            forward_copy(slot, side).wait()
    shared.wait()


def exchange(owners, sections, lesser, greater, coulomb):
    local, count, _, width = lesser.shape
    slots = count // owners
    energies = local * owners
    sides = 1 if sections == 2 else 2
    forward, inverse = tables(energies)
    split = (local, owners, slots, 2, width)
    tile_shape = jax.ShapeDtypeStruct(split, jnp.bfloat16)
    anywhere = pl.BlockSpec(memory_space=pl.ANY)
    near = pl.BlockSpec(memory_space=pltpu.VMEM)
    dma = pltpu.SemaphoreType.DMA
    return pl.pallas_call(
        functools.partial(
            exchange_kernel, owners, sections, 1.0 / (2 * energies * energies**0.5)
        ),
        in_specs=[anywhere] * 5,
        out_specs=[near] * (2 + sides),
        out_shape=[tile_shape] * (1 + sides)
        + [jax.ShapeDtypeStruct(coulomb.shape[1:], coulomb.dtype)],
        scratch_shapes=[
            pltpu.VMEM((slots, 2, energies, 2, width), jnp.bfloat16),
            pltpu.VMEM((slots, energies, 2, width), jnp.bfloat16),
            pltpu.VMEM(forward.shape, jnp.bfloat16),
            pltpu.VMEM(inverse.shape, jnp.bfloat16),
            dma((2,)),
            dma((slots,)),
            dma((slots,)),
            dma((slots,)),
            dma((slots,)),
            dma((sides, slots)),
            dma((sides, slots)),
            dma(()),
            dma(()),
        ],
        compiler_params=pltpu.CompilerParams(
            collective_id=0, has_side_effects=True, vmem_limit_bytes=VMEM_LIMIT
        ),
    )(lesser.reshape(split), greater.reshape(split), coulomb, forward, inverse)


def screen_setup(sections, coulomb_ref, other_ref, pattern_ref, right_ref, picked_ref, mask_ref):
    terms, count, nb = mask_ref.shape
    section = lax.axis_index("sec")
    lower = other_ref[...].astype(jnp.float32).T
    upper = coulomb_ref[1].astype(jnp.float32)
    matrices = [coulomb_ref[0].astype(jnp.float32)]
    if sections == 2:
        sources = [section, 1 - section]
        matrices.append(jnp.where(section == 0, upper, lower))
    else:
        sources = [
            section,
            lax.rem(section + sections - 1, sections),
            lax.rem(section + 1, sections),
        ]
        matrices.append(jnp.where(section > 0, lower, 0.0))
        matrices.append(jnp.where(section < sections - 1, upper, 0.0))
    position = lax.broadcasted_iota(jnp.int32, (nb, TR * count), 0)
    lane = lax.broadcasted_iota(jnp.int32, (count, nb), 1) // TC
    first = lax.broadcasted_iota(jnp.int32, (count, count), 0)
    second = lax.broadcasted_iota(jnp.int32, (count, count), 1)
    across = nb // TC
    for t in range(terms):
        listed = pattern_ref[pl.ds(sources[t], 1), :]
        row = jnp.concatenate([listed // across * TR + r for r in range(TR)], axis=1)
        chosen = jnp.where(position == row, 1.0, 0.0).astype(jnp.bfloat16)
        picked_ref[t] = dot32(matrices[t].astype(jnp.bfloat16), chosen).astype(jnp.bfloat16)
        column = jnp.sum(
            jnp.where(first == second, (listed % across).astype(jnp.float32), 0.0),
            axis=1,
            keepdims=True,
        ).astype(jnp.int32)
        mask_ref[t] = jnp.where(lane == column, 1.0, 0.0).astype(jnp.bfloat16)
        right_ref[t * nb : (t + 1) * nb] = matrices[t].T.astype(jnp.bfloat16)


def screen_kernel(sections, terms, batch, *refs):
    tile_refs = refs[:terms]
    coulomb_ref, other_ref, pattern_ref, out_ref = refs[terms : terms + 4]
    right_ref, picked_ref, mask_ref, rows_ref = refs[terms + 4 :]
    _, count, nb = mask_ref.shape
    width = rows_ref.shape[-1]

    @pl.when(pl.program_id(0) == 0)
    def _():
        screen_setup(
            sections, coulomb_ref, other_ref, pattern_ref, right_ref, picked_ref, mask_ref
        )

    lane = lax.broadcasted_iota(jnp.int32, (count, width), 1) % TC
    joined = [[] for _ in range(batch * 2)]
    for t in range(terms):
        for b in range(batch):
            rows_ref[t, b] = tile_refs[t][b].reshape(2 * count, width).astype(jnp.float32)
        mask = mask_ref[t]
        for b in range(batch):
            for c in range(2):
                tile = rows_ref[t, b, pl.ds(c, count, stride=2), :]
                pieces = []
                for r in range(TR):
                    spread = jnp.take_along_axis(
                        tile, lane + r * TC, axis=1, mode="promise_in_bounds"
                    )
                    spread = spread.astype(jnp.bfloat16)
                    wide = jnp.concatenate([spread] * (nb // width), axis=1)
                    pieces.append(wide * mask)
                stacked = jnp.concatenate(pieces, axis=0)
                joined[2 * b + c].append(dot32(picked_ref[t], stacked).astype(jnp.bfloat16))
    left = jnp.concatenate([jnp.concatenate(j, axis=1) for j in joined], axis=0)
    total = dot32(left, right_ref[...]).astype(jnp.bfloat16)
    out_ref[...] = total.reshape(batch, 2, nb, nb)


def screen(sections, tiles, coulomb, other, pattern):
    terms = len(tiles)
    energies, owners, slots, _, width = tiles[0].shape
    count = owners * slots
    nb = coulomb.shape[1]
    batch = next(n for n in (8, 4, 2, 1) if energies % n == 0)
    whole = lambda array: pl.BlockSpec(array.shape, lambda i: (0,) * array.ndim)
    return pl.pallas_call(
        functools.partial(screen_kernel, sections, terms, batch),
        grid=(energies // batch,),
        in_specs=[pl.BlockSpec((batch, owners, slots, 2, width), lambda i: (i, 0, 0, 0, 0))] * terms
        + [whole(coulomb), whole(other), whole(pattern)],
        out_specs=pl.BlockSpec((batch, 2, nb, nb), lambda i: (i, 0, 0, 0)),
        out_shape=jax.ShapeDtypeStruct((energies, 2, nb, nb), jnp.bfloat16),
        scratch_shapes=[
            pltpu.VMEM((terms * nb, nb), jnp.bfloat16),
            pltpu.VMEM((terms, nb, TR * count), jnp.bfloat16),
            pltpu.VMEM((terms, count, nb), jnp.bfloat16),
            pltpu.VMEM((terms, batch, 2 * count, width), jnp.float32),
        ],
        compiler_params=pltpu.CompilerParams(vmem_limit_bytes=VMEM_LIMIT),
    )(*tiles, coulomb, other, pattern)


def on_device(sections, owners, green_lesser, green_greater, coulomb, pattern):
    _, local, count, _, width = green_lesser.shape
    polar, *beside, other = exchange(
        owners, sections, green_lesser[0], green_greater[0], coulomb[0]
    )
    screened = screen(sections, [polar, *beside], coulomb[0], other, pattern)
    return polar.reshape(1, local, count, 2, width), screened[None]


def solution(mesh):
    in_specs = (
        P("sec", "el", None, None, None),
        P("sec", "el", None, None, None),
        P("sec", None, None, None),
        P(),
    )
    out_specs = (P("sec", "el", None, None, None), P("sec", "el", None, None, None))
    return jax.shard_map(
        functools.partial(on_device, mesh.shape["sec"], mesh.shape["el"]),
        mesh=mesh,
        in_specs=in_specs,
        out_specs=out_specs,
        check_vma=False,
    )
```

profile of v0, /device:TPU:0, one launch (start us, length us, event | category | flops | bytes accessed | tf_op | source)
XLA Modules:
  0.0 62.1 jit_solution(542567075840404639)
XLA Ops:
  0.6 50.3 %shard_map.77 = (bf16[16,16,4,2,128]{4,3,2,1,0:T(2,128)(2,1)}, bf16[16,16,4,2,128]{4,3,2,1,0:T(2,128)(2,1)}, bf16[256,256]{1,0:T(8,128)(2,1)}) custom-call(bf16[16,16,4,2,128]{4,3,2,1,0:T(2,128)(2,1)} %bitcast.9, bf16[16,16,4,2,128]{4,3,2,1,0:T(2,128)(2,1)} %bitcast.10, bf16[2,256,256]{2,1,0:T(8,128)(2,1)} %bitcast.7, ...), custom_call_target="tpu_custom_call" | custom-call | tf_op jit(solution)/shard_map/pallas_call | solution.py:224
  50.9 0.0 copy-start
  50.9 10.4 %shard_map.78 = bf16[16,2,256,256]{3,2,1,0:T(8,128)(2,1)} custom-call(bf16[16,16,4,2,128]{4,3,2,1,0:T(2,128)(2,1)} %get-tuple-element.5.refs_0_, bf16[16,16,4,2,128]{4,3,2,1,0:T(2,128)(2,1)} %get-tuple-element.6.refs_1_, bf16[2,256,256]{2,1,0:T(8,128)(2,1)} %bitcast.8, bf16[256,256]{1,0:T(8,128)(2,1)} %get-tuple-element.7.refs_3_, s32[2,64]{1,0:T(2,128)} %refs_4_.1), custom_call_target="tpu_custom_call" | custom-call | tf_op jit(solution)/shard_map/pallas_call | solution.py:333
  61.3 0.0 copy-done
  61.3 0.8 %copy.9 = bf16[1,16,64,2,128]{4,3,2,1,0:T(2,128)(2,1)} copy(bf16[1,16,64,2,128]{4,3,2,1,0:T(2,128)(2,1)S(1)} %bitcast.6) | data formatting | bytes 1048576
Async XLA Ops:
  50.9 10.4 %copy-start = (bf16[16,16,4,2,128]{4,3,2,1,0:T(2,128)(2,1)S(1)}, bf16[16,16,4,2,128]{4,3,2,1,0:T(2,128)(2,1)}, u32[]{:S(2)}) copy-start(bf16[16,16,4,2,128]{4,3,2,1,0:T(2,128)(2,1)} %get-tuple-element.5.refs_0_) | copy-start | bytes 1572868
where the time goes:
time: 62.3 us; the launch traced here: 62.1 us
  Pallas kernels  60.7 us (97%)
  local copies, waits for them, and re-layouts  0.8 us (1%)
  between operations  0.65 us (1%)
    pallas_call x1, Pallas kernels, exchange(): pl.pallas_call(functools.partial(exchange_kernel, owners, sections, 1.0 /...  50.3 us
    pallas_call x1, Pallas kernels, screen(): pl.pallas_call(functools.partial(screen_kernel, sections, terms, batch),...  10.4 us

commit v1 on v0

--- a/solution.py
+++ b/solution.py
@@ -13,47 +13,62 @@
 VMEM_LIMIT = 56 * 1024 * 1024
 
 
-def halves(table):
-    upper = table.astype(jnp.bfloat16)
-    lower = (table - upper.astype(np.float32)).astype(jnp.bfloat16)
-    return upper, lower
-
-
 def tables(energies):
-    length = 2 * energies
-    phase = np.outer(np.arange(length), np.arange(energies)) % length
+    length = energies
+    depth = energies // 2
+    order = np.concatenate([np.arange(0, length, 2), np.arange(1, length, 2)])
+    phase = np.outer(order, np.arange(depth)) % length
     phase = phase * (2.0 * np.pi / length)
     cosine = np.cos(phase).astype(np.float32)
     sine = np.sin(phase).astype(np.float32)
     real = np.stack([cosine, sine], axis=2).reshape(length, length)
     imag = np.stack([-sine, cosine], axis=2).reshape(length, length)
-    forward = np.concatenate(halves(np.concatenate([real, imag], axis=0)), axis=1)
+    forward = np.concatenate([real, imag], axis=0)
     out_r = np.concatenate([-sine.T, -cosine.T], axis=1)
     out_i = np.concatenate([cosine.T, -sine.T], axis=1)
     inverse = np.stack([out_r, out_i], axis=1).reshape(length, 2 * length)
-    return jnp.asarray(forward), jnp.asarray(np.concatenate(halves(inverse), axis=1))
+    return jnp.asarray(forward, jnp.bfloat16), jnp.asarray(inverse, jnp.bfloat16)
 
 
 def dot32(a, b):
     return jnp.dot(a, b, preferred_element_type=jnp.float32)
 
 
-def correlate_slot(factor, lesser, greater, forward_ref, inverse_ref):
-    energies, _, width = lesser.shape
-    length = 2 * energies
-    joined = jnp.concatenate(
-        [lesser.reshape(length, width), greater.reshape(length, width)], axis=1
+def conjugate_product(a, b):
+    (ar, ai), (br, bi) = a, b
+    return jnp.concatenate([ar * br + ai * bi, ai * br - ar * bi], axis=0).astype(jnp.bfloat16)
+
+
+def spectra(parts, forward_ref):
+    depth, _, width = parts[0].shape
+    length = 2 * depth
+    joined = jnp.concatenate([p.reshape(length, width) for p in parts], axis=1)
+    z = dot32(forward_ref[...], joined)
+    return [
+        (z[:length, i * width : (i + 1) * width], z[length:, i * width : (i + 1) * width])
+        for i in range(len(parts))
+    ]
+
+
+def low_part(factor, lesser, greater, forward_ref, inverse_ref):
+    first, second = spectra([lesser, greater], forward_ref)
+    return dot32(inverse_ref[...], conjugate_product(first, second)) * factor
+
+
+def high_parts(factor, lesser, below, greater, forward_ref, inverse_ref):
+    width = lesser.shape[-1]
+    first, under, second = spectra([lesser, below, greater], forward_ref)
+    middle = under[0].shape[0] // 2
+
+    def shifted(a, b):
+        return jnp.concatenate([b[:middle] + a[:middle], b[middle:] - a[middle:]], axis=0)
+
+    both = tuple(shifted(a, b) for a, b in zip(under, second))
+    product = jnp.concatenate(
+        [conjugate_product(first, both), conjugate_product(first, under)], axis=1
     )
-    z = dot32(forward_ref[:, :length], joined) + dot32(forward_ref[:, length:], joined)
-    lr, gr = z[:length, :width], z[:length, width:]
-    li, gi = z[length:, :width], z[length:, width:]
-    product = jnp.concatenate([lr * gr + li * gi, li * gr - lr * gi], axis=0)
-    high = product.astype(jnp.bfloat16)
-    low = (product - high.astype(jnp.float32)).astype(jnp.bfloat16)
-    depth = 2 * length
-    first = dot32(inverse_ref[:, :depth], jnp.concatenate([high, low], axis=1))
-    series = first[:, :width] + first[:, width:] + dot32(inverse_ref[:, depth:], high)
-    return (series * factor).astype(jnp.bfloat16).reshape(energies, 2, width)
+    series = dot32(inverse_ref[...], product) * factor
+    return series[:, :width], series[:, width:]
 
 
 def exchange_kernel(
@@ -63,8 +78,8 @@
     lesser_ref,
     greater_ref,
     coulomb_ref,
-    forward_hbm,
-    inverse_hbm,
+    forward_ref,
+    inverse_ref,
     *refs,
 ):
     sides = 1 if sections == 2 else 2
@@ -73,12 +88,18 @@
     other_ref = refs[1 + sides]
     (
         x_ref,
+        below_ref,
+        down_ref,
+        partial_ref,
         d_ref,
-        forward_ref,
-        inverse_ref,
-        table_sem,
         in_send,
         in_recv,
+        pass_send,
+        pass_recv,
+        up_send,
+        up_recv,
+        down_send,
+        down_recv,
         out_send,
         out_recv,
         side_send,
@@ -86,10 +107,18 @@
         c_send,
         c_recv,
     ) = refs[2 + sides :]
-    slots = x_ref.shape[0]
+    tiles = x_ref.shape[1]
     local = polar_ref.shape[0]
+    width = polar_ref.shape[-1]
+    group = owners // 4
+    half = owners // 2
     me = lax.axis_index("el")
     section = lax.axis_index("sec")
+    quarter = me // group
+    place = lax.rem(me, group)
+    base = quarter * group
+    half_base = (quarter // 2) * half
+    spot = lax.rem(me, half)
     mesh_id = pl.DeviceIdType.MESH
     if sections == 2:
         targets = [1 - section]
@@ -99,46 +128,77 @@
             lax.rem(section + sections - 1, sections),
         ]
 
-    load_f = pltpu.make_async_copy(forward_hbm, forward_ref, table_sem.at[0])
-    load_i = pltpu.make_async_copy(inverse_hbm, inverse_ref, table_sem.at[1])
-    load_f.start()
-    load_i.start()
-
     barrier = pltpu.get_barrier_semaphore()
 
     def greet(step, carry):
-        peer = lax.rem(me + step, owners)
+        peer = half_base + lax.rem(spot + step, half)
         pl.semaphore_signal(barrier, inc=1, device_id={"el": peer}, device_id_type=mesh_id)
         return carry
 
-    lax.fori_loop(1, owners, greet, 0)
+    lax.fori_loop(1, half, greet, 0)
     for target in targets:
         pl.semaphore_signal(barrier, inc=1, device_id={"sec": target}, device_id_type=mesh_id)
-    pl.semaphore_wait(barrier, owners - 1 + sides)
-
-    def peer_at(turn):
-        return lax.rem(me + 1 + turn, owners)
-
-    mine = pl.ds(me * local, local)
-    for slot in range(slots):
-        for which, source in enumerate((lesser_ref, greater_ref)):
-
-            def send(turn, carry, slot=slot, which=which, source=source):
-                peer = peer_at(turn)
-                pltpu.make_async_remote_copy(
-                    src_ref=source.at[:, peer, slot],
-                    dst_ref=x_ref.at[slot, which, mine],
-                    send_sem=in_send.at[slot],
-                    recv_sem=in_recv.at[slot],
-                    device_id={"el": peer},
-                    device_id_type=mesh_id,
-                ).start()
-                return carry
-
-            pltpu.make_async_copy(
-                source.at[:, me, slot], x_ref.at[slot, which, mine], in_recv.at[slot]
+
+    def greet_across(peer):
+        pl.semaphore_signal(barrier, inc=1, device_id={"el": peer}, device_id_type=mesh_id)
+        pl.semaphore_wait(barrier, half + sides)
+
+    @pl.when(quarter == 1)
+    def _():
+        greet_across(me + group)
+
+    @pl.when(quarter == 2)
+    def _():
+        greet_across(me - group)
+
+    @pl.when(jnp.logical_or(quarter == 0, quarter == 3))
+    def _():
+        pl.semaphore_wait(barrier, half - 1 + sides)
+
+    mine = pl.ds(spot * local, local)
+    own = pl.ds(lax.rem(quarter, 2) * group * local, group * local)
+    theirs = pl.ds((1 - lax.rem(quarter, 2)) * group * local, group * local)
+
+    def send_in(which, source, tile):
+        pltpu.make_async_copy(
+            source.at[:, place, tile], x_ref.at[which, tile, mine], in_recv.at[which, tile]
+        ).start()
+
+        def send(turn, carry):
+            peer = lax.rem(place + 1 + turn, group)
+            pltpu.make_async_remote_copy(
+                src_ref=source.at[:, peer, tile],
+                dst_ref=x_ref.at[which, tile, mine],
+                send_sem=in_send,
+                recv_sem=in_recv.at[which, tile],
+                device_id={"el": base + peer},
+                device_id_type=mesh_id,
             ).start()
-            lax.fori_loop(0, owners - 1, send, 0)
+            return carry
+
+        lax.fori_loop(0, group - 1, send, 0)
+
+    @pl.when(quarter < 2)
+    def _():
+        def send_g(tile, carry):
+            send_in(1, greater_ref, tile)
+            return carry
+
+        def send_l(tile, carry):
+            send_in(0, lesser_ref, tile)
+            return carry
+
+        lax.fori_loop(0, tiles, send_g, 0)
+        lax.fori_loop(0, tiles, send_l, 0)
+
+    @pl.when(quarter >= 2)
+    def _():
+        def send_both(tile, carry):
+            send_in(0, lesser_ref, tile)
+            send_in(1, greater_ref, tile)
+            return carry
+
+        lax.fori_loop(0, tiles, send_both, 0)
 
     shared = pltpu.make_async_remote_copy(
         src_ref=coulomb_ref.at[1],
@@ -149,98 +209,214 @@
         device_id_type=mesh_id,
     )
     shared.start()
-    load_f.wait()
-    load_i.wait()
-
-    def arrive(slot):
-        whole = polar_ref.at[:, :, slot]
-        pltpu.make_async_copy(whole, whole, out_recv.at[slot]).wait()
-
-    def forward_copy(slot, side):
+
+    def gathered(which, tile):
+        part = x_ref.at[which, tile, own]
+        pltpu.make_async_copy(part, part, in_recv.at[which, tile]).wait()
+
+    def pass_inward(which, tile, peer):
+        gathered(which, tile)
+        pltpu.make_async_remote_copy(
+            src_ref=x_ref.at[which, tile, own],
+            dst_ref=x_ref.at[which, tile, own],
+            send_sem=pass_send,
+            recv_sem=pass_recv.at[which, tile],
+            device_id={"el": peer},
+            device_id_type=mesh_id,
+        ).start()
+
+    def passed(which, tile):
+        part = x_ref.at[which, tile, theirs]
+        pltpu.make_async_copy(part, part, pass_recv.at[which, tile]).wait()
+
+    def forward_copy(tile, side):
         return pltpu.make_async_remote_copy(
-            src_ref=polar_ref.at[:, :, slot],
-            dst_ref=beside_refs[side].at[:, :, slot],
-            send_sem=side_send.at[side, slot],
-            recv_sem=side_recv.at[side, slot],
+            src_ref=polar_ref.at[:, :, tile],
+            dst_ref=beside_refs[side].at[:, :, tile],
+            send_sem=side_send.at[side, tile],
+            recv_sem=side_recv.at[side, tile],
             device_id={"sec": targets[side]},
             device_id_type=mesh_id,
         )
 
-    def pass_on(slot):
-        arrive(slot)
+    def pass_on(tile):
+        whole = polar_ref.at[:, :, tile]
+        pltpu.make_async_copy(whole, whole, out_recv.at[tile]).wait()
         for side in range(sides):
-            forward_copy(slot, side).start()
-
-    for slot in range(slots):
-        whole = x_ref.at[slot]
-        pltpu.make_async_copy(whole, whole, in_recv.at[slot]).wait()
-        d_ref[slot] = correlate_slot(
-            factor, x_ref[slot, 0], x_ref[slot, 1], forward_ref, inverse_ref
-        )
+            forward_copy(tile, side).start()
+
+    def give(tile):
         pltpu.make_async_copy(
-            d_ref.at[slot, mine], polar_ref.at[:, me, slot], out_recv.at[slot]
+            d_ref.at[tile, mine], polar_ref.at[:, place, tile], out_recv.at[tile]
         ).start()
 
-        def give(turn, carry, slot=slot):
-            peer = peer_at(turn)
+        def send(turn, carry):
+            peer = lax.rem(spot + 1 + turn, half)
             pltpu.make_async_remote_copy(
-                src_ref=d_ref.at[slot, pl.ds(peer * local, local)],
-                dst_ref=polar_ref.at[:, me, slot],
-                send_sem=out_send.at[slot],
-                recv_sem=out_recv.at[slot],
-                device_id={"el": peer},
+                src_ref=d_ref.at[tile, pl.ds(peer * local, local)],
+                dst_ref=polar_ref.at[:, place, tile],
+                send_sem=out_send,
+                recv_sem=out_recv.at[tile],
+                device_id={"el": half_base + peer},
                 device_id_type=mesh_id,
             ).start()
             return carry
 
-        lax.fori_loop(0, owners - 1, give, 0)
-        if slot >= 2:
-            pass_on(slot - 2)
-    for slot in range(max(slots - 2, 0), slots):
-        pass_on(slot)
-
-    sent = (owners - 1) * local
-    for slot in range(slots):
-        part = x_ref.at[slot, :, pl.ds(0, sent)]
-        pltpu.make_async_copy(part, part, in_send.at[slot]).wait()
-        part = d_ref.at[slot, pl.ds(0, sent)]
-        pltpu.make_async_copy(part, part, out_send.at[slot]).wait()
+        lax.fori_loop(0, half - 1, send, 0)
+
+    def outer(peer, pairs):
+        for order in pairs:
+
+            def step(tile, carry, order=order):
+                for which in order:
+                    pass_inward(which, tile, peer)
+                return carry
+
+            lax.fori_loop(0, tiles, step, 0)
+
+        def finish(tile, carry):
+            pass_on(tile)
+            return carry
+
+        lax.fori_loop(0, tiles, finish, 0)
+        part = x_ref.at[:, :, own]
+        pltpu.make_async_copy(part, part, pass_send).wait()
+
+    @pl.when(quarter == 0)
+    def _():
+        outer(me + group, [(1,), (0,)])
+
+    @pl.when(quarter == 3)
+    def _():
+        outer(me - group, [(0, 1)])
+
+    def late(step):
+        lag = 2
+
+        def body(tile, carry):
+            step(tile)
+
+            @pl.when(tile >= lag)
+            def _():
+                pass_on(tile - lag)
+
+            return carry
+
+        lax.fori_loop(0, tiles, body, 0)
+        for tile in range(max(tiles - lag, 0), tiles):
+            pass_on(tile)
+        sent = (half - 1) * local
+        part = d_ref.at[:, pl.ds(0, sent)]
+        pltpu.make_async_copy(part, part, out_send).wait()
+
+    @pl.when(quarter == 1)
+    def _():
+        def lift(tile, carry):
+            gathered(1, tile)
+            passed(1, tile)
+            pltpu.make_async_remote_copy(
+                src_ref=x_ref.at[1, tile],
+                dst_ref=below_ref.at[tile],
+                send_sem=up_send,
+                recv_sem=up_recv.at[tile],
+                device_id={"el": me + group},
+                device_id_type=mesh_id,
+            ).start()
+            return carry
+
+        lax.fori_loop(0, tiles, lift, 0)
+
+        def step(tile):
+            gathered(0, tile)
+            passed(0, tile)
+            value = low_part(factor, x_ref[0, tile], x_ref[1, tile], forward_ref, inverse_ref)
+            part = partial_ref.at[tile]
+            pltpu.make_async_copy(part, part, down_recv.at[tile]).wait()
+            value = value + partial_ref[tile].reshape(value.shape).astype(jnp.float32)
+            d_ref[tile] = value.astype(jnp.bfloat16).reshape(d_ref.shape[1:])
+            give(tile)
+
+        late(step)
+        pltpu.make_async_copy(below_ref, below_ref, up_send).wait()
+
+    @pl.when(quarter == 2)
+    def _():
+        def step(tile):
+            gathered(0, tile)
+            gathered(1, tile)
+            passed(0, tile)
+            passed(1, tile)
+            part = below_ref.at[tile]
+            pltpu.make_async_copy(part, part, up_recv.at[tile]).wait()
+            lower, upper = high_parts(
+                factor, x_ref[0, tile], below_ref[tile], x_ref[1, tile], forward_ref, inverse_ref
+            )
+            shape = d_ref.shape[1:]
+            down_ref[tile] = lower.astype(jnp.bfloat16).reshape(shape)
+            pltpu.make_async_remote_copy(
+                src_ref=down_ref.at[tile],
+                dst_ref=partial_ref.at[tile],
+                send_sem=down_send,
+                recv_sem=down_recv.at[tile],
+                device_id={"el": me - group},
+                device_id_type=mesh_id,
+            ).start()
+            d_ref[tile] = upper.astype(jnp.bfloat16).reshape(shape)
+            give(tile)
+
+        late(step)
+        pltpu.make_async_copy(down_ref, down_ref, down_send).wait()
+
+    part = x_ref.at[:, :, pl.ds(0, (group - 1) * local)]
+    pltpu.make_async_copy(part, part, in_send).wait()
+
+    def settle(tile, carry):
         for side in range(sides):
-            forward_copy(slot, side).wait()
+            forward_copy(tile, side).wait()
+        return carry
+
+    lax.fori_loop(0, tiles, settle, 0)
     shared.wait()
 
 
 def exchange(owners, sections, lesser, greater, coulomb):
     local, count, _, width = lesser.shape
-    slots = count // owners
+    group = owners // 4
+    tiles = count // group
     energies = local * owners
+    depth = energies // 2
     sides = 1 if sections == 2 else 2
     forward, inverse = tables(energies)
-    split = (local, owners, slots, 2, width)
+    split = (local, group, tiles, 2, width)
     tile_shape = jax.ShapeDtypeStruct(split, jnp.bfloat16)
     anywhere = pl.BlockSpec(memory_space=pl.ANY)
     near = pl.BlockSpec(memory_space=pltpu.VMEM)
     dma = pltpu.SemaphoreType.DMA
+    buffer = pltpu.VMEM((tiles, depth, 2, width), jnp.bfloat16)
     return pl.pallas_call(
-        functools.partial(
-            exchange_kernel, owners, sections, 1.0 / (2 * energies * energies**0.5)
-        ),
-        in_specs=[anywhere] * 5,
+        functools.partial(exchange_kernel, owners, sections, 1.0 / (energies * energies**0.5)),
+        in_specs=[anywhere] * 3 + [near] * 2,
         out_specs=[near] * (2 + sides),
         out_shape=[tile_shape] * (1 + sides)
         + [jax.ShapeDtypeStruct(coulomb.shape[1:], coulomb.dtype)],
         scratch_shapes=[
-            pltpu.VMEM((slots, 2, energies, 2, width), jnp.bfloat16),
-            pltpu.VMEM((slots, energies, 2, width), jnp.bfloat16),
-            pltpu.VMEM(forward.shape, jnp.bfloat16),
-            pltpu.VMEM(inverse.shape, jnp.bfloat16),
-            dma((2,)),
-            dma((slots,)),
-            dma((slots,)),
-            dma((slots,)),
-            dma((slots,)),
-            dma((sides, slots)),
-            dma((sides, slots)),
+            pltpu.VMEM((2, tiles, depth, 2, width), jnp.bfloat16),
+            buffer,
+            buffer,
+            buffer,
+            buffer,
+            dma(()),
+            dma((2, tiles)),
+            dma(()),
+            dma((2, tiles)),
+            dma(()),
+            dma((tiles,)),
+            dma(()),
+            dma((tiles,)),
+            dma(()),
+            dma((tiles,)),
+            dma((sides, tiles)),
+            dma((sides, tiles)),
             dma(()),
             dma(()),
         ],

time: 62.3 us -> 62.1 us (level)
  no operation moved by 1% of the time
where the time goes in v1:
time: 62.1 us; the launch traced here: 62 us
  Pallas kernels  60.5 us (97%)
  local copies, waits for them, and re-layouts  0.8 us (1%)
  between operations  0.65 us (1%)
    pallas_call x1, Pallas kernels, exchange(): pl.pallas_call(functools.partial(exchange_kernel, owners, sections, 1.0 /...  50.2 us
    pallas_call x1, Pallas kernels, screen(): pl.pallas_call(functools.partial(screen_kernel, sections, terms, batch),...  10.4 us

profile of v1, /device:TPU:0, one launch (start us, length us, event | category | flops | bytes accessed | tf_op | source)
XLA Modules:
  0.0 62.0 jit_solution(12635518259355839078)
XLA Ops:
  0.6 50.2 %shard_map.77 = (bf16[16,4,16,2,128]{4,3,2,1,0:T(2,128)(2,1)}, bf16[16,4,16,2,128]{4,3,2,1,0:T(2,128)(2,1)}, bf16[256,256]{1,0:T(8,128)(2,1)}) custom-call(bf16[16,4,16,2,128]{4,3,2,1,0:T(2,128)(2,1)} %bitcast.9, bf16[16,4,16,2,128]{4,3,2,1,0:T(2,128)(2,1)} %bitcast.10, bf16[2,256,256]{2,1,0:T(8,128)(2,1)} %bitcast.7, ...), custom_call_target="tpu_custom_call" | custom-call | tf_op jit(solution)/shard_map/pallas_call | solution.py:396
  50.8 0.0 copy-start
  50.8 10.4 %shard_map.78 = bf16[16,2,256,256]{3,2,1,0:T(8,128)(2,1)} custom-call(bf16[16,4,16,2,128]{4,3,2,1,0:T(2,128)(2,1)} %get-tuple-element.5.refs_0_, bf16[16,4,16,2,128]{4,3,2,1,0:T(2,128)(2,1)} %get-tuple-element.6.refs_1_, bf16[2,256,256]{2,1,0:T(8,128)(2,1)} %bitcast.8, bf16[256,256]{1,0:T(8,128)(2,1)} %get-tuple-element.7.refs_3_, s32[2,64]{1,0:T(2,128)} %refs_4_.1), custom_call_target="tpu_custom_call" | custom-call | tf_op jit(solution)/shard_map/pallas_call | solution.py:509
  61.2 0.0 copy-done
  61.2 0.8 %copy.9 = bf16[1,16,64,2,128]{4,3,2,1,0:T(2,128)(2,1)} copy(bf16[1,16,64,2,128]{4,3,2,1,0:T(2,128)(2,1)S(1)} %bitcast.6) | data formatting | bytes 1048576
Async XLA Ops:
  50.8 10.4 %copy-start = (bf16[16,4,16,2,128]{4,3,2,1,0:T(2,128)(2,1)S(1)}, bf16[16,4,16,2,128]{4,3,2,1,0:T(2,128)(2,1)}, u32[]{:S(2)}) copy-start(bf16[16,4,16,2,128]{4,3,2,1,0:T(2,128)(2,1)} %get-tuple-element.5.refs_0_) | copy-start | bytes 1572868

commit v2 on v1

v2 whole, which is shorter than its diff:
```python
import functools

import jax
import jax.numpy as jnp
import numpy as np
from jax import lax
from jax.experimental import pallas as pl
from jax.experimental.pallas import tpu as pltpu
from jax.sharding import PartitionSpec as P

TR = 8
TC = 16
VMEM_LIMIT = 56 * 1024 * 1024
GROUPS = 4
BATCHES = 4


def tables(energies):
    length = energies
    depth = energies // 2
    order = np.concatenate([np.arange(0, length, 2), np.arange(1, length, 2)])
    phase = np.outer(order, np.arange(depth)) % length
    phase = phase * (2.0 * np.pi / length)
    cosine = np.cos(phase).astype(np.float32)
    sine = np.sin(phase).astype(np.float32)
    real = np.stack([cosine, sine], axis=2).reshape(length, length)
    imag = np.stack([-sine, cosine], axis=2).reshape(length, length)
    forward = np.concatenate([real, imag], axis=0)
    out_r = np.concatenate([-sine.T, -cosine.T], axis=1)
    out_i = np.concatenate([cosine.T, -sine.T], axis=1)
    inverse = np.stack([out_r, out_i], axis=1).reshape(length, 2 * length)
    return jnp.asarray(forward, jnp.bfloat16), jnp.asarray(inverse, jnp.bfloat16)


def dot32(a, b):
    return jnp.dot(a, b, preferred_element_type=jnp.float32)


def conjugate_product(a, b):
    (ar, ai), (br, bi) = a, b
    return jnp.concatenate([ar * br + ai * bi, ai * br - ar * bi], axis=0).astype(jnp.bfloat16)


def spectra(parts, forward_ref):
    depth, _, width = parts[0].shape
    length = 2 * depth
    joined = jnp.concatenate([p.reshape(length, width) for p in parts], axis=1)
    z = dot32(forward_ref[...], joined)
    return [
        (z[:length, i * width : (i + 1) * width], z[length:, i * width : (i + 1) * width])
        for i in range(len(parts))
    ]


def low_part(factor, lesser, greater, forward_ref, inverse_ref):
    first, second = spectra([lesser, greater], forward_ref)
    return dot32(inverse_ref[...], conjugate_product(first, second)) * factor


def high_parts(factor, lesser, below, greater, forward_ref, inverse_ref):
    width = lesser.shape[-1]
    first, under, second = spectra([lesser, below, greater], forward_ref)
    middle = under[0].shape[0] // 2

    def shifted(a, b):
        return jnp.concatenate([b[:middle] + a[:middle], b[middle:] - a[middle:]], axis=0)

    both = tuple(shifted(a, b) for a, b in zip(under, second))
    product = jnp.concatenate(
        [conjugate_product(first, both), conjugate_product(first, under)], axis=1
    )
    series = dot32(inverse_ref[...], product) * factor
    return series[:, :width], series[:, width:]


def exchange_kernel(
    owners,
    sections,
    factor,
    lesser_ref,
    greater_ref,
    coulomb_ref,
    forward_ref,
    inverse_ref,
    pattern_ref,
    *refs,
):
    sides = 1 if sections == 2 else 2
    polar_ref = refs[0]
    beside_refs = refs[1 : 1 + sides]
    sum_hbm, right_ref, picked_last_ref, mask_last_ref = refs[1 + sides : 5 + sides]
    (
        other_ref,
        coulomb_near,
        sum_ref,
        picked_ref,
        mask_ref,
        rows_ref,
        low_ref,
        sum_sem,
        near_sem,
        x_ref,
        below_ref,
        down_ref,
        partial_ref,
        d_ref,
        in_send,
        in_recv,
        pass_send,
        pass_recv,
        up_send,
        up_recv,
        down_send,
        down_recv,
        out_send,
        out_recv,
        side_send,
        side_recv,
        c_send,
        c_recv,
    ) = refs[5 + sides :]
    tiles = x_ref.shape[1]
    local = polar_ref.shape[0]
    slots = tiles // GROUPS
    some = local // BATCHES
    group = owners // 4
    half = owners // 2
    me = lax.axis_index("el")
    section = lax.axis_index("sec")
    quarter = me // group
    place = lax.rem(me, group)
    base = quarter * group
    half_base = (quarter // 2) * half
    spot = lax.rem(me, half)
    outer = jnp.logical_or(quarter == 0, quarter == 3)
    inward = jnp.where(quarter == 0, me + group, me - group)
    mesh_id = pl.DeviceIdType.MESH
    if sections == 2:
        targets = [1 - section]
    else:
        targets = [
            lax.rem(section + 1, sections),
            lax.rem(section + sections - 1, sections),
        ]

    barrier = pltpu.get_barrier_semaphore()

    def greet(step, carry):
        peer = half_base + lax.rem(spot + step, half)
        pl.semaphore_signal(barrier, inc=1, device_id={"el": peer}, device_id_type=mesh_id)
        return carry

    lax.fori_loop(1, half, greet, 0)
    for target in targets:
        pl.semaphore_signal(barrier, inc=1, device_id={"sec": target}, device_id_type=mesh_id)

    def greet_across(peer):
        pl.semaphore_signal(barrier, inc=1, device_id={"el": peer}, device_id_type=mesh_id)
        pl.semaphore_wait(barrier, half + sides)

    @pl.when(quarter == 1)
    def _():
        greet_across(me + group)

    @pl.when(quarter == 2)
    def _():
        greet_across(me - group)

    @pl.when(outer)
    def _():
        pl.semaphore_wait(barrier, half - 1 + sides)

    mine = pl.ds(spot * local, local)
    own = pl.ds(lax.rem(quarter, 2) * group * local, group * local)
    theirs = pl.ds((1 - lax.rem(quarter, 2)) * group * local, group * local)

    def send_in(which, source, tile):
        pltpu.make_async_copy(
            source.at[:, place, tile], x_ref.at[which, tile, mine], in_recv.at[which, tile]
        ).start()

        def send(turn, carry):
            peer = lax.rem(place + 1 + turn, group)
            pltpu.make_async_remote_copy(
                src_ref=source.at[:, peer, tile],
                dst_ref=x_ref.at[which, tile, mine],
                send_sem=in_send,
                recv_sem=in_recv.at[which, tile],
                device_id={"el": base + peer},
                device_id_type=mesh_id,
            ).start()
            return carry

        lax.fori_loop(0, group - 1, send, 0)

    def send_both(tile, carry):
        send_in(1, greater_ref, tile)
        send_in(0, lesser_ref, tile)
        return carry

    lax.fori_loop(0, tiles, send_both, 0)

    shared = pltpu.make_async_remote_copy(
        src_ref=coulomb_ref.at[1],
        dst_ref=other_ref,
        send_sem=c_send,
        recv_sem=c_recv,
        device_id={"sec": targets[0]},
        device_id_type=mesh_id,
    )
    shared.start()

    def gathered(which, tile):
        part = x_ref.at[which, tile, own]
        pltpu.make_async_copy(part, part, in_recv.at[which, tile]).wait()

    def pass_inward(which, tile, peer):
        gathered(which, tile)
        pltpu.make_async_remote_copy(
            src_ref=x_ref.at[which, tile, own],
            dst_ref=x_ref.at[which, tile, own],
            send_sem=pass_send,
            recv_sem=pass_recv.at[which, tile],
            device_id={"el": peer},
            device_id_type=mesh_id,
        ).start()

    def passed(which, tile):
        part = x_ref.at[which, tile, theirs]
        pltpu.make_async_copy(part, part, pass_recv.at[which, tile]).wait()

    def forward_copy(tile, side):
        return pltpu.make_async_remote_copy(
            src_ref=polar_ref.at[:, :, tile],
            dst_ref=beside_refs[side].at[:, :, tile],
            send_sem=side_send.at[side, tile],
            recv_sem=side_recv.at[side, tile],
            device_id={"sec": targets[side]},
            device_id_type=mesh_id,
        )

    def pass_on(tile):
        whole = polar_ref.at[:, :, tile]
        pltpu.make_async_copy(whole, whole, out_recv.at[tile]).wait()
        for side in range(sides):
            forward_copy(tile, side).start()

    def give(tile):
        pltpu.make_async_copy(
            d_ref.at[tile, mine], polar_ref.at[:, place, tile], out_recv.at[tile]
        ).start()

        def send(turn, carry):
            peer = lax.rem(spot + 1 + turn, half)
            pltpu.make_async_remote_copy(
                src_ref=d_ref.at[tile, pl.ds(peer * local, local)],
                dst_ref=polar_ref.at[:, place, tile],
                send_sem=out_send,
                recv_sem=out_recv.at[tile],
                device_id={"el": half_base + peer},
                device_id_type=mesh_id,
            ).start()
            return carry

        lax.fori_loop(0, half - 1, send, 0)

    def lift(tile):
        gathered(1, tile)
        passed(1, tile)
        pltpu.make_async_remote_copy(
            src_ref=x_ref.at[1, tile],
            dst_ref=below_ref.at[tile],
            send_sem=up_send,
            recv_sem=up_recv.at[tile],
            device_id={"el": me + group},
            device_id_type=mesh_id,
        ).start()
        gathered(0, tile)
        passed(0, tile)
        low_ref[tile] = low_part(factor, x_ref[0, tile], x_ref[1, tile], forward_ref, inverse_ref)

    def complete(tile):
        part = partial_ref.at[tile]
        pltpu.make_async_copy(part, part, down_recv.at[tile]).wait()
        value = low_ref[tile]
        value = value + partial_ref[tile].reshape(value.shape).astype(jnp.float32)
        d_ref[tile] = value.astype(jnp.bfloat16).reshape(d_ref.shape[1:])
        give(tile)

    def upper(tile):
        gathered(0, tile)
        gathered(1, tile)
        passed(0, tile)
        passed(1, tile)
        part = below_ref.at[tile]
        pltpu.make_async_copy(part, part, up_recv.at[tile]).wait()
        down, above = high_parts(
            factor, x_ref[0, tile], below_ref[tile], x_ref[1, tile], forward_ref, inverse_ref
        )
        shape = d_ref.shape[1:]
        down_ref[tile] = down.astype(jnp.bfloat16).reshape(shape)
        pltpu.make_async_remote_copy(
            src_ref=down_ref.at[tile],
            dst_ref=partial_ref.at[tile],
            send_sem=down_send,
            recv_sem=down_recv.at[tile],
            device_id={"el": me - group},
            device_id_type=mesh_id,
        ).start()
        d_ref[tile] = above.astype(jnp.bfloat16).reshape(shape)
        give(tile)

    def prepare():
        pltpu.make_async_copy(coulomb_ref, coulomb_near, near_sem).wait()
        shared.wait_recv()
        screen_setup(
            sections,
            coulomb_near,
            other_ref,
            pattern_ref,
            right_ref,
            picked_ref,
            mask_ref,
            tiles,
        )
        picked_last_ref[...] = picked_ref[GROUPS - 1]
        mask_last_ref[...] = mask_ref[GROUPS - 1]
        for b in range(local):
            sum_ref[b] = jnp.zeros(sum_ref.shape[1:], sum_ref.dtype)

    def sum_copy(batch):
        part = pl.ds(batch * some, some)
        return pltpu.make_async_copy(sum_ref.at[part], sum_hbm.at[part], sum_sem.at[batch])

    def screen_some(turn):
        chunk = turn // BATCHES
        batch = lax.rem(turn, BATCHES)

        @pl.when(batch == 0)
        def _():
            for s in range(slots):
                for side in range(sides):
                    forward_copy(chunk * slots + s, side).wait_recv()

        start = batch * some
        columns = pl.ds(chunk * slots, slots)
        sources = [polar_ref, *beside_refs]
        for t in range(1 + sides):
            for b in range(some):
                piece = sources[t][start + b, :, columns]
                rows_ref[t, b] = piece.reshape(rows_ref.shape[2:]).astype(jnp.float32)
        masks = [mask_ref[chunk, t] for t in range(1 + sides)]
        added = screen_chunk(some, rows_ref, masks, right_ref, picked_ref[chunk])
        for b in range(some):
            for c in range(2):
                old = sum_ref[start + b, c].astype(jnp.float32)
                sum_ref[start + b, c] = (old + added[2 * b + c]).astype(jnp.bfloat16)

        @pl.when(chunk == GROUPS - 2)
        def _():
            sum_copy(batch).start()

    pltpu.make_async_copy(coulomb_ref, coulomb_near, near_sem).start()
    turns = (GROUPS - 1) * BATCHES
    lead = slots + 2
    last = max(tiles, turns + lead)
    behind = 6
    delay = jnp.where(outer, tiles, jnp.where(quarter == 1, behind + 2, 2))
    ready = jnp.where(outer, tiles, jnp.where(quarter == 1, 3, 0))

    def body(i, carry):
        @pl.when(jnp.logical_and(outer, i < tiles))
        def _():
            pass_inward(1, i, inward)
            pass_inward(0, i, inward)

        @pl.when(jnp.logical_and(quarter == 1, i < tiles))
        def _():
            lift(i)

        @pl.when(i == ready)
        def _():
            prepare()

        @pl.when(
            jnp.logical_and(quarter == 1, jnp.logical_and(i >= behind, i < tiles + behind))
        )
        def _():
            complete(i - behind)

        @pl.when(jnp.logical_and(quarter == 2, i < tiles))
        def _():
            upper(i)

        tile = i - delay

        @pl.when(jnp.logical_and(tile >= 0, tile < tiles))
        def _():
            pass_on(tile)

        turn = tile - lead

        @pl.when(jnp.logical_and(turn >= 0, turn < turns))
        def _():
            screen_some(turn)

        return carry

    lax.fori_loop(0, last + delay, body, 0)

    @pl.when(outer)
    def _():
        part = x_ref.at[:, :, own]
        pltpu.make_async_copy(part, part, pass_send).wait()

    @pl.when(jnp.logical_not(outer))
    def _():
        part = d_ref.at[:, pl.ds(0, (half - 1) * local)]
        pltpu.make_async_copy(part, part, out_send).wait()

    @pl.when(quarter == 1)
    def _():
        pltpu.make_async_copy(below_ref, below_ref, up_send).wait()

    @pl.when(quarter == 2)
    def _():
        pltpu.make_async_copy(down_ref, down_ref, down_send).wait()

    part = x_ref.at[:, :, pl.ds(0, (group - 1) * local)]
    pltpu.make_async_copy(part, part, in_send).wait()
    for batch in range(BATCHES):
        sum_copy(batch).wait()

    def settle_sent(tile, carry):
        for side in range(sides):
            forward_copy(tile, side).wait_send()
        return carry

    def settle(tile, carry):
        for side in range(sides):
            forward_copy(tile, side).wait()
        return carry

    lax.fori_loop(0, (GROUPS - 1) * slots, settle_sent, 0)
    lax.fori_loop((GROUPS - 1) * slots, tiles, settle, 0)
    shared.wait_send()


def exchange(owners, sections, lesser, greater, coulomb, pattern):
    local, count, _, width = lesser.shape
    group = owners // 4
    tiles = count // group
    energies = local * owners
    depth = energies // 2
    nb = coulomb.shape[1]
    sides = 1 if sections == 2 else 2
    terms = 1 + sides
    chunk = count // GROUPS
    forward, inverse = tables(energies)
    split = (local, group, tiles, 2, width)
    bf16 = jnp.bfloat16
    tile_shape = jax.ShapeDtypeStruct(split, bf16)
    anywhere = pl.BlockSpec(memory_space=pl.ANY)
    near = pl.BlockSpec(memory_space=pltpu.VMEM)
    dma = pltpu.SemaphoreType.DMA
    buffer = pltpu.VMEM((tiles, depth, 2, width), bf16)
    return pl.pallas_call(
        functools.partial(exchange_kernel, owners, sections, 1.0 / (energies * energies**0.5)),
        in_specs=[anywhere] * 3 + [near] * 3,
        out_specs=[near] * (1 + sides) + [anywhere] + [near] * 3,
        out_shape=[tile_shape] * (1 + sides)
        + [
            jax.ShapeDtypeStruct((local, 2, nb, nb), bf16),
            jax.ShapeDtypeStruct((terms, nb, nb), bf16),
            jax.ShapeDtypeStruct((nb, terms * TR * chunk), bf16),
            jax.ShapeDtypeStruct((terms, chunk, nb), bf16),
        ],
        scratch_shapes=[
            pltpu.VMEM((nb, nb), bf16),
            pltpu.VMEM(coulomb.shape, bf16),
            pltpu.VMEM((local, 2, nb, nb), bf16),
            pltpu.VMEM((GROUPS, nb, terms * TR * chunk), bf16),
            pltpu.VMEM((GROUPS, terms, chunk, nb), bf16),
            pltpu.VMEM((terms, local // BATCHES, 2 * chunk, width), jnp.float32),
            pltpu.VMEM((tiles, energies, width), jnp.float32),
            dma((BATCHES,)),
            dma(()),
            pltpu.VMEM((2, tiles, depth, 2, width), bf16),
            buffer,
            buffer,
            buffer,
            buffer,
            dma(()),
            dma((2, tiles)),
            dma(()),
            dma((2, tiles)),
            dma(()),
            dma((tiles,)),
            dma(()),
            dma((tiles,)),
            dma(()),
            dma((tiles,)),
            dma((sides, tiles)),
            dma((sides, tiles)),
            dma(()),
            dma(()),
        ],
        compiler_params=pltpu.CompilerParams(
            collective_id=0, has_side_effects=True, vmem_limit_bytes=VMEM_LIMIT
        ),
    )(lesser.reshape(split), greater.reshape(split), coulomb, forward, inverse, pattern)


def screen_setup(
    sections, coulomb_ref, other_ref, pattern_ref, right_ref, picked_ref, mask_ref, tiles
):
    groups, terms, chunk, nb = mask_ref.shape
    count = groups * chunk
    slots = tiles // groups
    section = lax.axis_index("sec")
    lower = other_ref[...].astype(jnp.float32).T
    upper = coulomb_ref[1].astype(jnp.float32)
    matrices = [coulomb_ref[0].astype(jnp.float32)]
    if sections == 2:
        sources = [section, 1 - section]
        matrices.append(jnp.where(section == 0, upper, lower))
    else:
        sources = [
            section,
            lax.rem(section + sections - 1, sections),
            lax.rem(section + 1, sections),
        ]
        matrices.append(jnp.where(section > 0, lower, 0.0))
        matrices.append(jnp.where(section < sections - 1, upper, 0.0))
    across = nb // TC
    wide = TR * count
    iota = lambda shape, axis: lax.broadcasted_iota(jnp.int32, shape, axis)
    row_of = iota((nb, wide), 0)
    lane = iota((count, wide), 1)
    member = lane % chunk
    listed_at = (member // slots) * tiles + lane // (TR * chunk) * slots + member % slots
    taken = listed_at == iota((count, wide), 0)
    inner_row = iota((1, wide), 1) // chunk % TR
    diagonal = iota((count, count), 0) == iota((count, count), 1)
    member = iota((chunk, count), 0)
    begin = (member // slots) * tiles + member % slots
    column_of = iota((chunk, nb), 1) // TC
    for t in range(terms):
        listed = pattern_ref[pl.ds(sources[t], 1), :].astype(jnp.float32)
        upright = jnp.sum(jnp.where(diagonal, listed, 0.0), axis=1, keepdims=True)
        spread = jnp.sum(jnp.where(taken, upright, 0.0), axis=0, keepdims=True).astype(jnp.int32)
        row = spread // across * TR + inner_row
        chosen = jnp.where(row_of == row, 1.0, 0.0).astype(jnp.bfloat16)
        picked = dot32(matrices[t].astype(jnp.bfloat16), chosen).astype(jnp.bfloat16)
        span = TR * chunk
        for g in range(groups):
            picked_ref[g, :, t * span : (t + 1) * span] = picked[:, g * span : (g + 1) * span]
            here = iota((chunk, count), 1) == begin + g * slots
            place = jnp.sum(jnp.where(here, listed, 0.0), axis=1, keepdims=True).astype(jnp.int32)
            mask_ref[g, t] = jnp.where(column_of == place % across, 1.0, 0.0).astype(jnp.bfloat16)
        right_ref[t] = matrices[t].T.astype(jnp.bfloat16)


def screen_chunk(batch, rows_ref, masks, right_ref, picked):
    terms = len(masks)
    chunk, nb = masks[0].shape
    width = rows_ref.shape[-1]
    lane = lax.broadcasted_iota(jnp.int32, (chunk, width), 1) % TC
    halves = []
    for t in range(terms):
        stacked = []
        for b in range(batch):
            for c in range(2):
                tile = rows_ref[t, b, pl.ds(c, chunk, stride=2), :]
                for r in range(TR):
                    spread = jnp.take_along_axis(
                        tile, lane + r * TC, axis=1, mode="promise_in_bounds"
                    ).astype(jnp.bfloat16)
                    stacked.append(jnp.concatenate([spread] * (nb // width), axis=1) * masks[t])
        stacked = jnp.concatenate(stacked, axis=0)
        halves.append(dot32(stacked, right_ref[t]).astype(jnp.bfloat16))
    span = TR * chunk
    added = []
    for n in range(2 * batch):
        part = jnp.concatenate([h[n * span : (n + 1) * span] for h in halves], axis=0)
        added.append(dot32(picked, part))
    return added


def screen_kernel(terms, batch, *refs):
    tile_refs = refs[:terms]
    polar_ref, sum_ref, right_ref, picked_ref, mask_ref = refs[terms : terms + 5]
    polar_out, out_ref, rows_ref = refs[terms + 5 :]
    polar_out[...] = polar_ref[...]
    for t in range(terms):
        for b in range(batch):
            rows_ref[t, b] = tile_refs[t][b].reshape(rows_ref.shape[2:]).astype(jnp.float32)
    masks = [mask_ref[t] for t in range(terms)]
    added = screen_chunk(batch, rows_ref, masks, right_ref, picked_ref[...])
    for b in range(batch):
        for c in range(2):
            out_ref[b, c] = (sum_ref[b, c].astype(jnp.float32) + added[2 * b + c]).astype(
                jnp.bfloat16
            )


def screen(tiles, total, right, picked, mask):
    terms = len(tiles)
    local, group, per, _, width = tiles[0].shape
    chunk, nb = mask.shape[1:]
    batch = local // BATCHES
    slots = per // GROUPS
    whole = lambda array: pl.BlockSpec(array.shape, lambda i: (0,) * array.ndim)
    some = pl.BlockSpec((batch, group, slots, 2, width), lambda i: (i, 0, GROUPS - 1, 0, 0))
    full = pl.BlockSpec((batch, group, per, 2, width), lambda i: (i, 0, 0, 0, 0))
    square = pl.BlockSpec((batch, 2, nb, nb), lambda i: (i, 0, 0, 0))
    return pl.pallas_call(
        functools.partial(screen_kernel, terms, batch),
        grid=(BATCHES,),
        in_specs=[some] * terms + [full, square, whole(right), whole(picked), whole(mask)],
        out_specs=[full, square],
        out_shape=[
            jax.ShapeDtypeStruct(tiles[0].shape, jnp.bfloat16),
            jax.ShapeDtypeStruct(total.shape, jnp.bfloat16),
        ],
        scratch_shapes=[pltpu.VMEM((terms, batch, 2 * chunk, width), jnp.float32)],
        compiler_params=pltpu.CompilerParams(vmem_limit_bytes=VMEM_LIMIT),
    )(*tiles, tiles[0], total, right, picked, mask)


def on_device(sections, owners, green_lesser, green_greater, coulomb, pattern):
    _, local, count, _, width = green_lesser.shape
    sides = 1 if sections == 2 else 2
    results = exchange(
        owners, sections, green_lesser[0], green_greater[0], coulomb[0], pattern
    )
    polar, screened = screen(results[: 1 + sides], *results[1 + sides :])
    return polar.reshape(1, local, count, 2, width), screened[None]


def solution(mesh):
    in_specs = (
        P("sec", "el", None, None, None),
        P("sec", "el", None, None, None),
        P("sec", None, None, None),
        P(),
    )
    out_specs = (P("sec", "el", None, None, None), P("sec", "el", None, None, None))
    return jax.shard_map(
        functools.partial(on_device, mesh.shape["sec"], mesh.shape["el"]),
        mesh=mesh,
        in_specs=in_specs,
        out_specs=out_specs,
        check_vma=False,
    )
```

time: 62.1 us -> 59.4 us (0.957)
  Pallas kernels: 60.5 us -> 58.5 us
  local copies, waits for them, and re-layouts: 0.8 us -> 0 us
    pallas_call x1, Pallas kernels: 10.4 us -> 6.69 us  [screen(): pl.pallas_call(functools.partial(screen_kernel, terms, batch), grid=(BATC...]
    pallas_call x1, Pallas kernels: 50.2 us -> 51.8 us  [exchange(): pl.pallas_call(functools.partial(exchange_kernel, owners, sections, 1.0 /...]
    unnamed x3 -> x0, local copies, waits for them, and re-layouts: 0.8 us -> none
where the time goes in v2:
time: 59.4 us; the launch traced here: 59.1 us
  Pallas kernels  58.5 us (98%)
  between operations  0.64 us (1%)
    pallas_call x1, Pallas kernels, exchange(): pl.pallas_call(functools.partial(exchange_kernel, owners, sections, 1.0 /...  51.8 us
    pallas_call x1, Pallas kernels, screen(): pl.pallas_call(functools.partial(screen_kernel, terms, batch), grid=(BATC...  6.69 us

profile of v2, /device:TPU:0, one launch (start us, length us, event | category | flops | bytes accessed | tf_op | source)
XLA Modules:
  0.0 59.1 jit_solution(16487170697158353230)
XLA Ops:
  0.6 51.8 %shard_map.77 = (bf16[16,4,16,2,128]{4,3,2,1,0:T(2,128)(2,1)}, bf16[16,4,16,2,128]{4,3,2,1,0:T(2,128)(2,1)}, bf16[16,2,256,256]{3,2,1,0:T(8,128)(2,1)}, bf16[2,2...) custom-call(bf16[16,4,16,2,128]{4,3,2,1,0:T(2,128)(2,1)} %bitcast.5, ...), custom_call_target="tpu_custom_call" | custom-call | tf_op jit(solution)/shard_map/pallas_call | solution.py:467
  52.4 6.7 %shard_map.78 = (bf16[16,4,16,2,128]{4,3,2,1,0:T(2,128)(2,1)}, bf16[16,2,256,256]{3,2,1,0:T(8,128)(2,1)}) custom-call(bf16[16,4,16,2,128]{4,3,2,1,0:T(2,128)(2,1)} %get-tuple-element.10.refs_0_.refs_2_, bf16[16,4,16,2,128]{4,3,2,1,0:T(2,128)(2,1)} %get-tuple-element.11.refs_1_, bf16[16,4,16,2,128]{4,3,2,1,0:T(2,128)(2,1)} %get-tuple-element.10.refs_0_.refs_2_, ...), custom_call_target="tpu_custom_call" | custom-call | tf_op jit(solution)/shard_map/pallas_call | solution.py:617

commit v3 on v2

--- a/solution.py
+++ b/solution.py
@@ -12,7 +12,7 @@
 TC = 16
 VMEM_LIMIT = 56 * 1024 * 1024
 GROUPS = 4
-BATCHES = 4
+BATCHES = 2
 
 
 def tables(energies):
@@ -80,8 +80,8 @@
     lesser_ref,
     greater_ref,
     coulomb_ref,
-    forward_ref,
-    inverse_ref,
+    forward_hbm,
+    inverse_hbm,
     pattern_ref,
     *refs,
 ):
@@ -90,13 +90,15 @@
     beside_refs = refs[1 : 1 + sides]
     sum_hbm, right_ref, picked_last_ref, mask_last_ref = refs[1 + sides : 5 + sides]
     (
+        forward_ref,
+        inverse_ref,
+        table_sem,
         other_ref,
         coulomb_near,
         sum_ref,
         picked_ref,
         mask_ref,
         rows_ref,
-        low_ref,
         sum_sem,
         near_sem,
         x_ref,
@@ -143,6 +145,10 @@
             lax.rem(section + sections - 1, sections),
         ]
 
+    load_f = pltpu.make_async_copy(forward_hbm, forward_ref, table_sem.at[0])
+    load_i = pltpu.make_async_copy(inverse_hbm, inverse_ref, table_sem.at[1])
+    load_f.start()
+    load_i.start()
     barrier = pltpu.get_barrier_semaphore()
 
     def greet(step, carry):
@@ -154,21 +160,19 @@
     for target in targets:
         pl.semaphore_signal(barrier, inc=1, device_id={"sec": target}, device_id_type=mesh_id)
 
-    def greet_across(peer):
-        pl.semaphore_signal(barrier, inc=1, device_id={"el": peer}, device_id_type=mesh_id)
-        pl.semaphore_wait(barrier, half + sides)
-
-    @pl.when(quarter == 1)
+    @pl.when(quarter < 2)
     def _():
-        greet_across(me + group)
+        for peer in range(group):
+            pl.semaphore_signal(
+                barrier, inc=1, device_id={"el": half + peer}, device_id_type=mesh_id
+            )
 
     @pl.when(quarter == 2)
     def _():
-        greet_across(me - group)
-
-    @pl.when(outer)
-    def _():
-        pl.semaphore_wait(barrier, half - 1 + sides)
+        pl.semaphore_signal(barrier, inc=1, device_id={"el": me - group}, device_id_type=mesh_id)
+
+    greeted = jnp.where(quarter == 2, half, jnp.where(quarter == 1, 1, 0))
+    pl.semaphore_wait(barrier, half - 1 + sides + greeted)
 
     mine = pl.ds(spot * local, local)
     own = pl.ds(lax.rem(quarter, 2) * group * local, group * local)
@@ -191,7 +195,8 @@
             ).start()
             return carry
 
-        lax.fori_loop(0, group - 1, send, 0)
+        for turn in range(group - 1):
+            send(turn, 0)
 
     def send_both(tile, carry):
         send_in(1, greater_ref, tile)
@@ -242,6 +247,15 @@
     def pass_on(tile):
         whole = polar_ref.at[:, :, tile]
         pltpu.make_async_copy(whole, whole, out_recv.at[tile]).wait()
+
+        @pl.when(quarter < 2)
+        def _():
+            part = partial_ref.at[:, :, tile]
+            pltpu.make_async_copy(part, part, down_recv.at[tile]).wait()
+            both = polar_ref[:, :, tile].astype(jnp.float32)
+            both = both + partial_ref[:, :, tile].astype(jnp.float32)
+            polar_ref[:, :, tile] = both.astype(jnp.bfloat16)
+
         for side in range(sides):
             forward_copy(tile, side).start()
 
@@ -262,7 +276,8 @@
             ).start()
             return carry
 
-        lax.fori_loop(0, half - 1, send, 0)
+        for turn in range(half - 1):
+            send(turn, 0)
 
     def lift(tile):
         gathered(1, tile)
@@ -277,13 +292,7 @@
         ).start()
         gathered(0, tile)
         passed(0, tile)
-        low_ref[tile] = low_part(factor, x_ref[0, tile], x_ref[1, tile], forward_ref, inverse_ref)
-
-    def complete(tile):
-        part = partial_ref.at[tile]
-        pltpu.make_async_copy(part, part, down_recv.at[tile]).wait()
-        value = low_ref[tile]
-        value = value + partial_ref[tile].reshape(value.shape).astype(jnp.float32)
+        value = low_part(factor, x_ref[0, tile], x_ref[1, tile], forward_ref, inverse_ref)
         d_ref[tile] = value.astype(jnp.bfloat16).reshape(d_ref.shape[1:])
         give(tile)
 
@@ -299,14 +308,15 @@
         )
         shape = d_ref.shape[1:]
         down_ref[tile] = down.astype(jnp.bfloat16).reshape(shape)
-        pltpu.make_async_remote_copy(
-            src_ref=down_ref.at[tile],
-            dst_ref=partial_ref.at[tile],
-            send_sem=down_send,
-            recv_sem=down_recv.at[tile],
-            device_id={"el": me - group},
-            device_id_type=mesh_id,
-        ).start()
+        for peer in range(half):
+            pltpu.make_async_remote_copy(
+                src_ref=down_ref.at[tile, peer * local : (peer + 1) * local],
+                dst_ref=partial_ref.at[:, place, tile],
+                send_sem=down_send,
+                recv_sem=down_recv.at[tile],
+                device_id={"el": peer},
+                device_id_type=mesh_id,
+            ).start()
         d_ref[tile] = above.astype(jnp.bfloat16).reshape(shape)
         give(tile)
 
@@ -361,11 +371,14 @@
             sum_copy(batch).start()
 
     pltpu.make_async_copy(coulomb_ref, coulomb_near, near_sem).start()
+    load_f.wait()
+    load_i.wait()
     turns = (GROUPS - 1) * BATCHES
     lead = slots + 2
-    last = max(tiles, turns + lead)
+    stride = max(1, slots // BATCHES)
+    last = max(tiles, (turns - 1) * stride + 1 + lead)
     behind = 6
-    delay = jnp.where(outer, tiles, jnp.where(quarter == 1, behind + 2, 2))
+    delay = jnp.where(outer, tiles, jnp.where(quarter == 1, behind, 2))
     ready = jnp.where(outer, tiles, jnp.where(quarter == 1, 3, 0))
 
     def body(i, carry):
@@ -382,25 +395,22 @@
         def _():
             prepare()
 
+        @pl.when(jnp.logical_and(quarter == 2, i < tiles))
+        def _():
+            upper(i)
+
+        tile = i - delay
+
+        @pl.when(jnp.logical_and(tile >= 0, tile < tiles))
+        def _():
+            pass_on(tile)
+
+        since = tile - lead
+        turn = since // stride
+
         @pl.when(
-            jnp.logical_and(quarter == 1, jnp.logical_and(i >= behind, i < tiles + behind))
+            jnp.logical_and(since >= 0, jnp.logical_and(since % stride == 0, turn < turns))
         )
-        def _():
-            complete(i - behind)
-
-        @pl.when(jnp.logical_and(quarter == 2, i < tiles))
-        def _():
-            upper(i)
-
-        tile = i - delay
-
-        @pl.when(jnp.logical_and(tile >= 0, tile < tiles))
-        def _():
-            pass_on(tile)
-
-        turn = tile - lead
-
-        @pl.when(jnp.logical_and(turn >= 0, turn < turns))
         def _():
             screen_some(turn)
 
@@ -466,7 +476,7 @@
     buffer = pltpu.VMEM((tiles, depth, 2, width), bf16)
     return pl.pallas_call(
         functools.partial(exchange_kernel, owners, sections, 1.0 / (energies * energies**0.5)),
-        in_specs=[anywhere] * 3 + [near] * 3,
+        in_specs=[anywhere] * 5 + [near],
         out_specs=[near] * (1 + sides) + [anywhere] + [near] * 3,
         out_shape=[tile_shape] * (1 + sides)
         + [
@@ -476,19 +486,21 @@
             jax.ShapeDtypeStruct((terms, chunk, nb), bf16),
         ],
         scratch_shapes=[
+            pltpu.VMEM(forward.shape, bf16),
+            pltpu.VMEM(inverse.shape, bf16),
+            dma((2,)),
             pltpu.VMEM((nb, nb), bf16),
             pltpu.VMEM(coulomb.shape, bf16),
             pltpu.VMEM((local, 2, nb, nb), bf16),
             pltpu.VMEM((GROUPS, nb, terms * TR * chunk), bf16),
             pltpu.VMEM((GROUPS, terms, chunk, nb), bf16),
             pltpu.VMEM((terms, local // BATCHES, 2 * chunk, width), jnp.float32),
-            pltpu.VMEM((tiles, energies, width), jnp.float32),
             dma((BATCHES,)),
             dma(()),
             pltpu.VMEM((2, tiles, depth, 2, width), bf16),
             buffer,
             buffer,
-            buffer,
+            pltpu.VMEM(split, bf16),
             buffer,
             dma(()),
             dma((2, tiles)),

time: 59.4 us -> 55.4 us (0.933)
  Pallas kernels: 58.5 us -> 54.5 us
    pallas_call x1, Pallas kernels: 51.8 us -> 48.5 us  [exchange(): pl.pallas_call(functools.partial(exchange_kernel, owners, sections, 1.0 /...]
    pallas_call x1, Pallas kernels: 6.69 us -> 6.03 us  [screen(): pl.pallas_call(functools.partial(screen_kernel, terms, batch), grid=(BATC...]
where the time goes in v3:
time: 55.4 us; the launch traced here: 55.2 us
  Pallas kernels  54.5 us (98%)
  between operations  0.64 us (1%)
    pallas_call x1, Pallas kernels, exchange(): pl.pallas_call(functools.partial(exchange_kernel, owners, sections, 1.0 /...  48.5 us
    pallas_call x1, Pallas kernels, screen(): pl.pallas_call(functools.partial(screen_kernel, terms, batch), grid=(BATC...  6.03 us

profile of v3, /device:TPU:0, one launch (start us, length us, event | category | flops | bytes accessed | tf_op | source)
XLA Modules:
  0.0 55.2 jit_solution(3535523752839595921)
XLA Ops:
  0.6 48.5 %shard_map.77 = (bf16[16,4,16,2,128]{4,3,2,1,0:T(2,128)(2,1)}, bf16[16,4,16,2,128]{4,3,2,1,0:T(2,128)(2,1)}, bf16[16,2,256,256]{3,2,1,0:T(8,128)(2,1)}, bf16[2,2...) custom-call(bf16[16,4,16,2,128]{4,3,2,1,0:T(2,128)(2,1)} %bitcast.5, ...), custom_call_target="tpu_custom_call" | custom-call | tf_op jit(solution)/shard_map/pallas_call | solution.py:477
  49.2 6.0 %shard_map.78 = (bf16[16,4,16,2,128]{4,3,2,1,0:T(2,128)(2,1)}, bf16[16,2,256,256]{3,2,1,0:T(8,128)(2,1)}) custom-call(bf16[16,4,16,2,128]{4,3,2,1,0:T(2,128)(2,1)} %get-tuple-element.10.refs_0_.refs_2_, bf16[16,4,16,2,128]{4,3,2,1,0:T(2,128)(2,1)} %get-tuple-element.11.refs_1_, bf16[16,4,16,2,128]{4,3,2,1,0:T(2,128)(2,1)} %get-tuple-element.10.refs_0_.refs_2_, ...), custom_call_target="tpu_custom_call" | custom-call | tf_op jit(solution)/shard_map/pallas_call | solution.py:629

commit v4 on v3

--- a/solution.py
+++ b/solution.py
@@ -10,9 +10,10 @@
 
 TR = 8
 TC = 16
-VMEM_LIMIT = 56 * 1024 * 1024
+VMEM_LIMIT = 40 * 1024 * 1024
 GROUPS = 4
 BATCHES = 2
+STEPS = 4
 
 
 def tables(energies):
@@ -82,24 +83,23 @@
     coulomb_ref,
     forward_hbm,
     inverse_hbm,
-    pattern_ref,
+    pattern_hbm,
     *refs,
 ):
     sides = 1 if sections == 2 else 2
     polar_ref = refs[0]
     beside_refs = refs[1 : 1 + sides]
-    sum_hbm, right_ref, picked_last_ref, mask_last_ref = refs[1 + sides : 5 + sides]
+    sum_ref, right_ref, picked_last_ref, mask_last_ref = refs[1 + sides : 5 + sides]
     (
+        pattern_ref,
         forward_ref,
         inverse_ref,
         table_sem,
         other_ref,
         coulomb_near,
-        sum_ref,
         picked_ref,
         mask_ref,
         rows_ref,
-        sum_sem,
         near_sem,
         x_ref,
         below_ref,
@@ -147,8 +147,10 @@
 
     load_f = pltpu.make_async_copy(forward_hbm, forward_ref, table_sem.at[0])
     load_i = pltpu.make_async_copy(inverse_hbm, inverse_ref, table_sem.at[1])
+    load_p = pltpu.make_async_copy(pattern_hbm, pattern_ref, table_sem.at[2])
     load_f.start()
     load_i.start()
+    load_p.start()
     barrier = pltpu.get_barrier_semaphore()
 
     def greet(step, carry):
@@ -338,10 +340,6 @@
         for b in range(local):
             sum_ref[b] = jnp.zeros(sum_ref.shape[1:], sum_ref.dtype)
 
-    def sum_copy(batch):
-        part = pl.ds(batch * some, some)
-        return pltpu.make_async_copy(sum_ref.at[part], sum_hbm.at[part], sum_sem.at[batch])
-
     def screen_some(turn):
         chunk = turn // BATCHES
         batch = lax.rem(turn, BATCHES)
@@ -366,19 +364,16 @@
                 old = sum_ref[start + b, c].astype(jnp.float32)
                 sum_ref[start + b, c] = (old + added[2 * b + c]).astype(jnp.bfloat16)
 
-        @pl.when(chunk == GROUPS - 2)
-        def _():
-            sum_copy(batch).start()
-
     pltpu.make_async_copy(coulomb_ref, coulomb_near, near_sem).start()
     load_f.wait()
     load_i.wait()
+    load_p.wait()
     turns = (GROUPS - 1) * BATCHES
-    lead = slots + 2
+    lead = slots + 1
     stride = max(1, slots // BATCHES)
     last = max(tiles, (turns - 1) * stride + 1 + lead)
     behind = 6
-    delay = jnp.where(outer, tiles, jnp.where(quarter == 1, behind, 2))
+    delay = jnp.where(outer, tiles, jnp.where(quarter == 1, behind, 3))
     ready = jnp.where(outer, tiles, jnp.where(quarter == 1, 3, 0))
 
     def body(i, carry):
@@ -438,8 +433,6 @@
 
     part = x_ref.at[:, :, pl.ds(0, (group - 1) * local)]
     pltpu.make_async_copy(part, part, in_send).wait()
-    for batch in range(BATCHES):
-        sum_copy(batch).wait()
 
     def settle_sent(tile, carry):
         for side in range(sides):
@@ -469,33 +462,32 @@
     forward, inverse = tables(energies)
     split = (local, group, tiles, 2, width)
     bf16 = jnp.bfloat16
-    tile_shape = jax.ShapeDtypeStruct(split, bf16)
-    anywhere = pl.BlockSpec(memory_space=pl.ANY)
+    far = pl.BlockSpec(memory_space=pltpu.HBM)
     near = pl.BlockSpec(memory_space=pltpu.VMEM)
     dma = pltpu.SemaphoreType.DMA
     buffer = pltpu.VMEM((tiles, depth, 2, width), bf16)
+    operands = [lesser.reshape(split), greater.reshape(split), coulomb, forward, inverse, pattern]
     return pl.pallas_call(
         functools.partial(exchange_kernel, owners, sections, 1.0 / (energies * energies**0.5)),
-        in_specs=[anywhere] * 5 + [near],
-        out_specs=[near] * (1 + sides) + [anywhere] + [near] * 3,
-        out_shape=[tile_shape] * (1 + sides)
+        in_specs=[far] * 6,
+        out_specs=[near] * (5 + sides),
+        out_shape=[pltpu.VMEM(split, bf16)] * (1 + sides)
         + [
-            jax.ShapeDtypeStruct((local, 2, nb, nb), bf16),
-            jax.ShapeDtypeStruct((terms, nb, nb), bf16),
-            jax.ShapeDtypeStruct((nb, terms * TR * chunk), bf16),
-            jax.ShapeDtypeStruct((terms, chunk, nb), bf16),
+            pltpu.VMEM((local, 2, nb, nb), bf16),
+            pltpu.VMEM((terms, nb, nb), bf16),
+            pltpu.VMEM((nb, terms * TR * chunk), bf16),
+            pltpu.VMEM((terms, chunk, nb), bf16),
         ],
         scratch_shapes=[
+            pltpu.VMEM(pattern.shape, pattern.dtype),
             pltpu.VMEM(forward.shape, bf16),
             pltpu.VMEM(inverse.shape, bf16),
-            dma((2,)),
+            dma((3,)),
             pltpu.VMEM((nb, nb), bf16),
             pltpu.VMEM(coulomb.shape, bf16),
-            pltpu.VMEM((local, 2, nb, nb), bf16),
             pltpu.VMEM((GROUPS, nb, terms * TR * chunk), bf16),
             pltpu.VMEM((GROUPS, terms, chunk, nb), bf16),
             pltpu.VMEM((terms, local // BATCHES, 2 * chunk, width), jnp.float32),
-            dma((BATCHES,)),
             dma(()),
             pltpu.VMEM((2, tiles, depth, 2, width), bf16),
             buffer,
@@ -520,7 +512,7 @@
         compiler_params=pltpu.CompilerParams(
             collective_id=0, has_side_effects=True, vmem_limit_bytes=VMEM_LIMIT
         ),
-    )(lesser.reshape(split), greater.reshape(split), coulomb, forward, inverse, pattern)
+    )(*[pltpu.with_memory_space_constraint(array, pltpu.HBM) for array in operands])
 
 
 def screen_setup(
@@ -573,25 +565,27 @@
         right_ref[t] = matrices[t].T.astype(jnp.bfloat16)
 
 
+def right_part(batch, rows, mask, right):
+    chunk, nb = mask.shape
+    width = rows.shape[-1]
+    lane = lax.broadcasted_iota(jnp.int32, (chunk, width), 1) % TC
+    stacked = []
+    for b in range(batch):
+        for c in range(2):
+            tile = rows[b, pl.ds(c, chunk, stride=2), :]
+            for r in range(TR):
+                spread = jnp.take_along_axis(
+                    tile, lane + r * TC, axis=1, mode="promise_in_bounds"
+                ).astype(jnp.bfloat16)
+                stacked.append(jnp.concatenate([spread] * (nb // width), axis=1) * mask)
+    return dot32(jnp.concatenate(stacked, axis=0), right).astype(jnp.bfloat16)
+
+
 def screen_chunk(batch, rows_ref, masks, right_ref, picked):
-    terms = len(masks)
-    chunk, nb = masks[0].shape
-    width = rows_ref.shape[-1]
-    lane = lax.broadcasted_iota(jnp.int32, (chunk, width), 1) % TC
-    halves = []
-    for t in range(terms):
-        stacked = []
-        for b in range(batch):
-            for c in range(2):
-                tile = rows_ref[t, b, pl.ds(c, chunk, stride=2), :]
-                for r in range(TR):
-                    spread = jnp.take_along_axis(
-                        tile, lane + r * TC, axis=1, mode="promise_in_bounds"
-                    ).astype(jnp.bfloat16)
-                    stacked.append(jnp.concatenate([spread] * (nb // width), axis=1) * masks[t])
-        stacked = jnp.concatenate(stacked, axis=0)
-        halves.append(dot32(stacked, right_ref[t]).astype(jnp.bfloat16))
-    span = TR * chunk
+    span = TR * masks[0].shape[0]
+    halves = [
+        right_part(batch, rows_ref.at[t], mask, right_ref[t]) for t, mask in enumerate(masks)
+    ]
     added = []
     for n in range(2 * batch):
         part = jnp.concatenate([h[n * span : (n + 1) * span] for h in halves], axis=0)
@@ -601,43 +595,77 @@
 
 def screen_kernel(terms, batch, *refs):
     tile_refs = refs[:terms]
-    polar_ref, sum_ref, right_ref, picked_ref, mask_ref = refs[terms : terms + 5]
-    polar_out, out_ref, rows_ref = refs[terms + 5 :]
-    polar_out[...] = polar_ref[...]
-    for t in range(terms):
+    sum_ref, right_ref, picked_ref, mask_ref, polar_out, out_hbm = refs[terms : terms + 6]
+    total_ref, rows_ref, half_ref, keep_sem, total_sem = refs[terms + 6 :]
+    polar_ref = tile_refs[0]
+    local, _, per, _, _ = polar_ref.shape
+    slots = per // GROUPS
+    steps = local // batch
+    def store(step):
+        part = pl.ds(step * batch, batch)
+        return pltpu.make_async_copy(total_ref.at[part], out_hbm.at[part], total_sem.at[step])
+
+    keep = pltpu.make_async_copy(polar_ref, polar_out, keep_sem)
+    keep.start()
+    masks = [mask_ref[t] for t in range(terms)]
+
+    span = TR * mask_ref.shape[1]
+    wide = local // max(1, local // 16)
+
+    def fill(step, carry):
+        for t in range(terms):
+            for b in range(wide):
+                e = step * wide + b
+                piece = tile_refs[t][e, :, per - slots :]
+                rows_ref[t, b] = piece.reshape(rows_ref.shape[2:]).astype(jnp.float32)
+            half = right_part(wide, rows_ref.at[t], masks[t], right_ref[t])
+            half_ref[pl.ds(step * wide * 2, wide * 2), t * span : (t + 1) * span] = half.reshape(
+                wide * 2, span, half.shape[-1]
+            )
+        return carry
+
+    lax.fori_loop(0, local // wide, fill, 0)
+
+    def body(step, carry):
         for b in range(batch):
-            rows_ref[t, b] = tile_refs[t][b].reshape(rows_ref.shape[2:]).astype(jnp.float32)
-    masks = [mask_ref[t] for t in range(terms)]
-    added = screen_chunk(batch, rows_ref, masks, right_ref, picked_ref[...])
-    for b in range(batch):
-        for c in range(2):
-            out_ref[b, c] = (sum_ref[b, c].astype(jnp.float32) + added[2 * b + c]).astype(
-                jnp.bfloat16
-            )
+            for c in range(2):
+                e = step * batch + b
+                total = dot32(picked_ref[...], half_ref[2 * e + c])
+                total = total + sum_ref[e, c].astype(jnp.float32)
+                total_ref[e, c] = total.astype(jnp.bfloat16)
+        store(step).start()
+        return carry
+
+    for step in range(steps):
+        body(step, 0)
+    keep.wait()
+    for step in range(steps):
+        store(step).wait()
 
 
 def screen(tiles, total, right, picked, mask):
     terms = len(tiles)
-    local, group, per, _, width = tiles[0].shape
-    chunk, nb = mask.shape[1:]
-    batch = local // BATCHES
-    slots = per // GROUPS
-    whole = lambda array: pl.BlockSpec(array.shape, lambda i: (0,) * array.ndim)
-    some = pl.BlockSpec((batch, group, slots, 2, width), lambda i: (i, 0, GROUPS - 1, 0, 0))
-    full = pl.BlockSpec((batch, group, per, 2, width), lambda i: (i, 0, 0, 0, 0))
-    square = pl.BlockSpec((batch, 2, nb, nb), lambda i: (i, 0, 0, 0))
+    local, _, _, _, width = tiles[0].shape
+    chunk = mask.shape[1]
+    batch = max(1, local // STEPS)
+    dma = pltpu.SemaphoreType.DMA
     return pl.pallas_call(
         functools.partial(screen_kernel, terms, batch),
-        grid=(BATCHES,),
-        in_specs=[some] * terms + [full, square, whole(right), whole(picked), whole(mask)],
-        out_specs=[full, square],
+        in_specs=[pl.BlockSpec(memory_space=pltpu.VMEM)] * (terms + 4),
+        out_specs=[pl.BlockSpec(memory_space=pltpu.HBM)] * 2,
         out_shape=[
             jax.ShapeDtypeStruct(tiles[0].shape, jnp.bfloat16),
-            jax.ShapeDtypeStruct(total.shape, jnp.bfloat16),
+            jax.ShapeDtypeStruct(total.shape, total.dtype),
         ],
-        scratch_shapes=[pltpu.VMEM((terms, batch, 2 * chunk, width), jnp.float32)],
+        scratch_shapes=[
+            pltpu.VMEM(total.shape, total.dtype),
+            pltpu.VMEM((terms, local, 2 * chunk, width), jnp.float32),
+            pltpu.VMEM((2 * local, terms * TR * chunk, total.shape[-1]), jnp.bfloat16),
+            dma(()),
+            dma((local // batch,)),
+        ],
         compiler_params=pltpu.CompilerParams(vmem_limit_bytes=VMEM_LIMIT),
-    )(*tiles, tiles[0], total, right, picked, mask)
+    )(*tiles, total, right, picked, mask)
 
 
 def on_device(sections, owners, green_lesser, green_greater, coulomb, pattern):

time: 55.4 us -> 51.4 us (0.928)
  Pallas kernels: 54.5 us -> 50.6 us
    pallas_call x1, Pallas kernels: 6.03 us -> 3.87 us  [screen(): pl.pallas_call(functools.partial(screen_kernel, terms, batch), in_specs=[...]
    pallas_call x1, Pallas kernels: 48.5 us -> 46.8 us  [exchange(): pl.pallas_call(functools.partial(exchange_kernel, owners, sections, 1.0 /...]
where the time goes in v4:
time: 51.4 us; the launch traced here: 51.3 us
  Pallas kernels  50.6 us (98%)
  between operations  0.64 us (1%)
    pallas_call x1, Pallas kernels, exchange(): pl.pallas_call(functools.partial(exchange_kernel, owners, sections, 1.0 /...  46.8 us
    pallas_call x1, Pallas kernels, screen(): pl.pallas_call(functools.partial(screen_kernel, terms, batch), in_specs=[...  3.87 us

profile of v4, /device:TPU:0, one launch (start us, length us, event | category | flops | bytes accessed | tf_op | source)
XLA Modules:
  0.0 51.3 jit_solution(5570126330159371267)
XLA Ops:
  0.6 46.8 %shard_map.77 = (bf16[16,4,16,2,128]{4,3,2,1,0:T(2,128)(2,1)S(1)}, bf16[16,4,16,2,128]{4,3,2,1,0:T(2,128)(2,1)S(1)}, bf16[16,2,256,256]{3,2,1,0:T(8,128)(2,1)S(1...) custom-call(bf16[16,4,16,2,128]{4,3,2,1,0:T(2,128)(2,1)} %bitcast.5, ...), custom_call_target="tpu_custom_call" | custom-call | tf_op jit(solution)/shard_map/pallas_call | solution.py:470
  47.4 3.9 %shard_map.78 = (bf16[16,4,16,2,128]{4,3,2,1,0:T(2,128)(2,1)}, bf16[16,2,256,256]{3,2,1,0:T(8,128)(2,1)}) custom-call(bf16[16,4,16,2,128]{4,3,2,1,0:T(2,128)(2,1)S(1)} %get-tuple-element.10.refs_0_, bf16[16,4,16,2,128]{4,3,2,1,0:T(2,128)(2,1)S(1)} %get-tuple-element.11.refs_1_, bf16[16,2,256,256]{3,2,1,0:T(8,128)(2,1)S(1)} %get-tuple-element.12.refs_2_, ...), custom_call_target="tpu_custom_call" | custom-call | tf_op jit(solution)/shard_map/pallas_call | solution.py:652

commit v5 on v4

--- a/solution.py
+++ b/solution.py
@@ -14,6 +14,7 @@
 GROUPS = 4
 BATCHES = 2
 STEPS = 4
+LEADS = (1, 1, 4)
 
 
 def tables(energies):
@@ -369,11 +370,11 @@
     load_i.wait()
     load_p.wait()
     turns = (GROUPS - 1) * BATCHES
-    lead = slots + 1
     stride = max(1, slots // BATCHES)
-    last = max(tiles, (turns - 1) * stride + 1 + lead)
     behind = 6
     delay = jnp.where(outer, tiles, jnp.where(quarter == 1, behind, 3))
+    lead = slots + jnp.where(outer, LEADS[0], jnp.where(quarter == 1, LEADS[1], LEADS[2]))
+    last = jnp.maximum(tiles, (turns - 1) * stride + 1 + lead)
     ready = jnp.where(outer, tiles, jnp.where(quarter == 1, 3, 0))
 
     def body(i, carry):

time: 51.4 us -> 49.9 us (0.971)
  Pallas kernels: 50.6 us -> 49.1 us
    pallas_call x1, Pallas kernels: 46.8 us -> 45.2 us  [exchange(): pl.pallas_call(functools.partial(exchange_kernel, owners, sections, 1.0 /...]
where the time goes in v5:
time: 49.9 us; the launch traced here: 49.7 us
  Pallas kernels  49.1 us (98%)
  between operations  0.64 us (1%)
    pallas_call x1, Pallas kernels, exchange(): pl.pallas_call(functools.partial(exchange_kernel, owners, sections, 1.0 /...  45.2 us
    pallas_call x1, Pallas kernels, screen(): pl.pallas_call(functools.partial(screen_kernel, terms, batch), in_specs=[...  3.87 us

profile of v5, /device:TPU:0, one launch (start us, length us, event | category | flops | bytes accessed | tf_op | source)
XLA Modules:
  0.0 49.7 jit_solution(8944434038137865228)
XLA Ops:
  0.6 45.2 %shard_map.77 = (bf16[16,4,16,2,128]{4,3,2,1,0:T(2,128)(2,1)S(1)}, bf16[16,4,16,2,128]{4,3,2,1,0:T(2,128)(2,1)S(1)}, bf16[16,2,256,256]{3,2,1,0:T(8,128)(2,1)S(1...) custom-call(bf16[16,4,16,2,128]{4,3,2,1,0:T(2,128)(2,1)} %bitcast.5, ...), custom_call_target="tpu_custom_call" | custom-call | tf_op jit(solution)/shard_map/pallas_call | solution.py:471
  45.9 3.9 %shard_map.78 = (bf16[16,4,16,2,128]{4,3,2,1,0:T(2,128)(2,1)}, bf16[16,2,256,256]{3,2,1,0:T(8,128)(2,1)}) custom-call(bf16[16,4,16,2,128]{4,3,2,1,0:T(2,128)(2,1)S(1)} %get-tuple-element.10.refs_0_, bf16[16,4,16,2,128]{4,3,2,1,0:T(2,128)(2,1)S(1)} %get-tuple-element.11.refs_1_, bf16[16,2,256,256]{3,2,1,0:T(8,128)(2,1)S(1)} %get-tuple-element.12.refs_2_, ...), custom_call_target="tpu_custom_call" | custom-call | tf_op jit(solution)/shard_map/pallas_call | solution.py:653

commit v6 on v5

--- a/solution.py
+++ b/solution.py
@@ -13,7 +13,7 @@
 VMEM_LIMIT = 40 * 1024 * 1024
 GROUPS = 4
 BATCHES = 2
-STEPS = 4
+STEPS = 8
 LEADS = (1, 1, 4)
 
 
@@ -90,9 +90,10 @@
     sides = 1 if sections == 2 else 2
     polar_ref = refs[0]
     beside_refs = refs[1 : 1 + sides]
-    sum_ref, right_ref, picked_last_ref, mask_last_ref = refs[1 + sides : 5 + sides]
+    sum_ref, right_ref, picked_last_ref, mask_last_ref, ours_ref = refs[1 + sides : 6 + sides]
     (
         pattern_ref,
+        last_ref,
         forward_ref,
         inverse_ref,
         table_sem,
@@ -121,7 +122,7 @@
         side_recv,
         c_send,
         c_recv,
-    ) = refs[5 + sides :]
+    ) = refs[6 + sides :]
     tiles = x_ref.shape[1]
     local = polar_ref.shape[0]
     slots = tiles // GROUPS
@@ -413,6 +414,11 @@
         return carry
 
     lax.fori_loop(0, last + delay, body, 0)
+    for b in range(local):
+        piece = polar_ref[b, :, tiles - slots :]
+        last_ref[b] = piece.reshape(last_ref.shape[1:]).astype(jnp.float32)
+    ours = right_part(local, last_ref, mask_ref[GROUPS - 1, 0], right_ref[0])
+    ours_ref[...] = ours.reshape(ours_ref.shape)
 
     @pl.when(outer)
     def _():
@@ -471,16 +477,18 @@
     return pl.pallas_call(
         functools.partial(exchange_kernel, owners, sections, 1.0 / (energies * energies**0.5)),
         in_specs=[far] * 6,
-        out_specs=[near] * (5 + sides),
+        out_specs=[near] * (6 + sides),
         out_shape=[pltpu.VMEM(split, bf16)] * (1 + sides)
         + [
             pltpu.VMEM((local, 2, nb, nb), bf16),
             pltpu.VMEM((terms, nb, nb), bf16),
             pltpu.VMEM((nb, terms * TR * chunk), bf16),
             pltpu.VMEM((terms, chunk, nb), bf16),
+            pltpu.VMEM((2 * local, TR * chunk, nb), bf16),
         ],
         scratch_shapes=[
             pltpu.VMEM(pattern.shape, pattern.dtype),
+            pltpu.VMEM((local, 2 * chunk, width), jnp.float32),
             pltpu.VMEM(forward.shape, bf16),
             pltpu.VMEM(inverse.shape, bf16),
             dma((3,)),
@@ -596,8 +604,8 @@
 
 def screen_kernel(terms, batch, *refs):
     tile_refs = refs[:terms]
-    sum_ref, right_ref, picked_ref, mask_ref, polar_out, out_hbm = refs[terms : terms + 6]
-    total_ref, rows_ref, half_ref, keep_sem, total_sem = refs[terms + 6 :]
+    sum_ref, right_ref, picked_ref, mask_ref, ours_ref, polar_out, out_hbm = refs[terms : terms + 7]
+    total_ref, rows_ref, half_ref, keep_sem, total_sem = refs[terms + 7 :]
     polar_ref = tile_refs[0]
     local, _, per, _, _ = polar_ref.shape
     slots = per // GROUPS
@@ -614,13 +622,13 @@
     wide = local // max(1, local // 16)
 
     def fill(step, carry):
-        for t in range(terms):
+        for t in range(1, terms):
             for b in range(wide):
                 e = step * wide + b
                 piece = tile_refs[t][e, :, per - slots :]
                 rows_ref[t, b] = piece.reshape(rows_ref.shape[2:]).astype(jnp.float32)
             half = right_part(wide, rows_ref.at[t], masks[t], right_ref[t])
-            half_ref[pl.ds(step * wide * 2, wide * 2), t * span : (t + 1) * span] = half.reshape(
+            half_ref[pl.ds(step * wide * 2, wide * 2), (t - 1) * span : t * span] = half.reshape(
                 wide * 2, span, half.shape[-1]
             )
         return carry
@@ -631,7 +639,8 @@
         for b in range(batch):
             for c in range(2):
                 e = step * batch + b
-                total = dot32(picked_ref[...], half_ref[2 * e + c])
+                part = jnp.concatenate([ours_ref[2 * e + c], half_ref[2 * e + c]], axis=0)
+                total = dot32(picked_ref[...], part)
                 total = total + sum_ref[e, c].astype(jnp.float32)
                 total_ref[e, c] = total.astype(jnp.bfloat16)
         store(step).start()
@@ -644,7 +653,7 @@
         store(step).wait()
 
 
-def screen(tiles, total, right, picked, mask):
+def screen(tiles, total, right, picked, mask, ours):
     terms = len(tiles)
     local, _, _, _, width = tiles[0].shape
     chunk = mask.shape[1]
@@ -652,7 +661,7 @@
     dma = pltpu.SemaphoreType.DMA
     return pl.pallas_call(
         functools.partial(screen_kernel, terms, batch),
-        in_specs=[pl.BlockSpec(memory_space=pltpu.VMEM)] * (terms + 4),
+        in_specs=[pl.BlockSpec(memory_space=pltpu.VMEM)] * (terms + 5),
         out_specs=[pl.BlockSpec(memory_space=pltpu.HBM)] * 2,
         out_shape=[
             jax.ShapeDtypeStruct(tiles[0].shape, jnp.bfloat16),
@@ -661,12 +670,12 @@
         scratch_shapes=[
             pltpu.VMEM(total.shape, total.dtype),
             pltpu.VMEM((terms, local, 2 * chunk, width), jnp.float32),
-            pltpu.VMEM((2 * local, terms * TR * chunk, total.shape[-1]), jnp.bfloat16),
+            pltpu.VMEM((2 * local, (terms - 1) * TR * chunk, total.shape[-1]), jnp.bfloat16),
             dma(()),
             dma((local // batch,)),
         ],
         compiler_params=pltpu.CompilerParams(vmem_limit_bytes=VMEM_LIMIT),
-    )(*tiles, total, right, picked, mask)
+    )(*tiles, total, right, picked, mask, ours)
 
 
 def on_device(sections, owners, green_lesser, green_greater, coulomb, pattern):

time: 49.9 us -> 49.3 us (0.988)
  Pallas kernels: 49.1 us -> 48.5 us
    pallas_call x1, Pallas kernels: 3.87 us -> 3.03 us  [screen(): pl.pallas_call(functools.partial(screen_kernel, terms, batch), in_specs=[...]
where the time goes in v6:
time: 49.3 us; the launch traced here: 49.1 us
  Pallas kernels  48.5 us (98%)
  between operations  0.64 us (1%)
    pallas_call x1, Pallas kernels, exchange(): pl.pallas_call(functools.partial(exchange_kernel, owners, sections, 1.0 /...  45.4 us
    pallas_call x1, Pallas kernels, screen(): pl.pallas_call(functools.partial(screen_kernel, terms, batch), in_specs=[...  3.03 us

profile of v6, /device:TPU:0, one launch (start us, length us, event | category | flops | bytes accessed | tf_op | source)
XLA Modules:
  0.0 49.1 jit_solution(7251548534429133040)
XLA Ops:
  0.6 45.4 %shard_map.77 = (bf16[16,4,16,2,128]{4,3,2,1,0:T(2,128)(2,1)S(1)}, bf16[16,4,16,2,128]{4,3,2,1,0:T(2,128)(2,1)S(1)}, bf16[16,2,256,256]{3,2,1,0:T(8,128)(2,1)S(1...) custom-call(bf16[16,4,16,2,128]{4,3,2,1,0:T(2,128)(2,1)} %bitcast.5,, ...), custom_call_target="tpu_custom_call" | custom-call | tf_op jit(solution)/shard_map/pallas_call | solution.py:477
  46.1 3.0 %shard_map.78 = (bf16[16,4,16,2,128]{4,3,2,1,0:T(2,128)(2,1)}, bf16[16,2,256,256]{3,2,1,0:T(8,128)(2,1)}) custom-call(bf16[16,4,16,2,128]{4,3,2,1,0:T(2,128)(2,1)S(1)} %get-tuple-element.11.refs_0_, bf16[16,4,16,2,128]{4,3,2,1,0:T(2,128)(2,1)S(1)} %get-tuple-element.12.refs_1_, bf16[16,2,256,256]{3,2,1,0:T(8,128)(2,1)S(1)} %get-tuple-element.13.refs_2_, ...), custom_call_target="tpu_custom_call" | custom-call | tf_op jit(solution)/shard_map/pallas_call | solution.py:662

commit v7 on v6

--- a/solution.py
+++ b/solution.py
@@ -14,7 +14,7 @@
 GROUPS = 4
 BATCHES = 2
 STEPS = 8
-LEADS = (1, 1, 4)
+LEADS = (1, 1, 3)
 
 
 def tables(energies):
@@ -373,7 +373,7 @@
     turns = (GROUPS - 1) * BATCHES
     stride = max(1, slots // BATCHES)
     behind = 6
-    delay = jnp.where(outer, tiles, jnp.where(quarter == 1, behind, 3))
+    delay = jnp.where(outer, tiles, jnp.where(quarter == 1, behind, 4))
     lead = slots + jnp.where(outer, LEADS[0], jnp.where(quarter == 1, LEADS[1], LEADS[2]))
     last = jnp.maximum(tiles, (turns - 1) * stride + 1 + lead)
     ready = jnp.where(outer, tiles, jnp.where(quarter == 1, 3, 0))

time: 49.3 us -> 49.3 us (level)
  no operation moved by 1% of the time
where the time goes in v7:
time: 49.3 us; the launch traced here: 49.1 us
  Pallas kernels  48.5 us (98%)
  between operations  0.64 us (1%)
    pallas_call x1, Pallas kernels, exchange(): pl.pallas_call(functools.partial(exchange_kernel, owners, sections, 1.0 /...  45.4 us
    pallas_call x1, Pallas kernels, screen(): pl.pallas_call(functools.partial(screen_kernel, terms, batch), in_specs=[...  3.03 us

profile of v7, /device:TPU:0, one launch (start us, length us, event | category | flops | bytes accessed | tf_op | source)
XLA Modules:
  0.0 49.1 jit_solution(6506286545372457642)
XLA Ops:
  0.6 45.4 %shard_map.77 = (bf16[16,4,16,2,128]{4,3,2,1,0:T(2,128)(2,1)S(1)}, bf16[16,4,16,2,128]{4,3,2,1,0:T(2,128)(2,1)S(1)}, bf16[16,2,256,256]{3,2,1,0:T(8,128)(2,1)S(1...) custom-call(bf16[16,4,16,2,128]{4,3,2,1,0:T(2,128)(2,1)} %bitcast.5,, ...), custom_call_target="tpu_custom_call" | custom-call | tf_op jit(solution)/shard_map/pallas_call | solution.py:477
  46.1 3.0 %shard_map.78 = (bf16[16,4,16,2,128]{4,3,2,1,0:T(2,128)(2,1)}, bf16[16,2,256,256]{3,2,1,0:T(8,128)(2,1)}) custom-call(bf16[16,4,16,2,128]{4,3,2,1,0:T(2,128)(2,1)S(1)} %get-tuple-element.11.refs_0_, bf16[16,4,16,2,128]{4,3,2,1,0:T(2,128)(2,1)S(1)} %get-tuple-element.12.refs_1_, bf16[16,2,256,256]{3,2,1,0:T(8,128)(2,1)S(1)} %get-tuple-element.13.refs_2_, ...), custom_call_target="tpu_custom_call" | custom-call | tf_op jit(solution)/shard_map/pallas_call | solution.py:662
